TPU v7x, 128 devices: a whole 4x4x4 slice. The times are simulated.
128 devices in a mesh: dp: 64 (over z, y, x), expert: 2 (over core).
Axes of the slice: x: 4, y: 4, z: 4, core: 2. Of those that a mesh axis runs over, the one named last changes fastest.
Arguments:
- hidden: bfloat16 [2, 65536, 1024], P('expert', 'dp'), may hold values from -6 to 6
- cotangent: bfloat16 [2, 65536, 3584], P('expert', 'dp'), may hold values from -6 to 6
- counts: int32 [2, 64], P('expert', 'dp'), may hold values from 1 to 1024, as said below
- placement: int32 [2, 4], replicated, may hold values from 0 to 1, as said below
- weight: bfloat16 [2, 1024, 3584], P('expert', 'dp'), may hold values from -4 to 4
- moment: float32 [2, 1024, 3584], P('expert', 'dp'), may hold values from -2 to 2
- second: float32 [2, 1024, 3584], P('expert', 'dp'), may hold values from 0.005 to 1
- serving: bfloat16 [2, 4, 1024, 3584], P('expert', None, 'dp'), may hold values from -4 to 4
Outputs:
- d_hidden: bfloat16 [2, 65536, 1024], P('expert', 'dp')
- new_weight: bfloat16 [2, 1024, 3584], P('expert', 'dp')
- new_moment: float32 [2, 1024, 3584], P('expert', 'dp')
- new_second: float32 [2, 1024, 3584], P('expert', 'dp')
- served: bfloat16 [2, 4, 1024, 3584], P('expert', None, 'dp')
Inputs may be any that keep to these rules, and one draw needn't show every extreme that they name: `counts`: every count is reached by some expert and data shard in every draw at its upper end, 1024. `placement`: some two groups hold different experts as their first replica.
All inputs are finite; a program needn't handle non-finite values.
Results may differ from a plain program's by a relative error of at most 0.0012.
Values may be sent and summed in bfloat16 or wider, within the bound.
A program may use at most 128 MiB of HBM per device.

v0:
```python
import jax
import jax.numpy as jnp
from jax import lax
from jax.sharding import Mesh
from jax.sharding import PartitionSpec as P

D = 3584
DP = ("dp_0", "dp_1", "dp_2")


beta_one = 0.9
beta_two = 0.95
bias_one = 1.0 - 0.9**20
bias_two = 1.0 - 0.95**20
learn_rate = 0.05
decay_rate = 0.1
epsilon = 1e-08


def summed_rows(array, axes, dim):
    if not axes:
        return array
    nearer = lax.psum_scatter(array, axes[0], scatter_dimension=dim, tiled=True)
    return summed_rows(nearer, axes[1:], dim)


def on_device(hidden, cotangent, counts, placement, weight, moment, second, serving):
    scale = D ** (-0.5)
    acts = hidden[0]
    grads_out = cotangent[0]
    matrix = weight[0]
    tokens = acts.shape[0]
    owned = matrix.shape[0]
    width = matrix.shape[1]
    live = jnp.arange(tokens, dtype=jnp.int32) < counts[0, 0]
    masked = jnp.where(live[:, None], grads_out, jnp.zeros_like(grads_out))
    d_full = scale * jnp.dot(
        masked, lax.all_gather(matrix, DP, axis=0, tiled=True).T, preferred_element_type=jnp.float32
    )
    d_hid = d_full.astype(jnp.bfloat16)
    full_term = scale * jnp.dot(acts.T, masked, preferred_element_type=jnp.float32)
    grad = summed_rows(full_term, DP, 0)
    first_new = beta_one * moment[0] + (1.0 - beta_one) * grad
    squares_new = beta_two * second[0] + (1.0 - beta_two) * grad * grad
    step = first_new / bias_one / (jnp.sqrt(squares_new / bias_two) + epsilon)
    current = matrix.astype(jnp.float32)
    updated = current - learn_rate * (step + decay_rate * current)
    delta = (updated - current).astype(jnp.bfloat16)
    groups = lax.axis_size("expert")
    flat = delta.reshape(groups, -1)
    spread = lax.all_to_all(flat, "expert", split_axis=0, concat_axis=0, tiled=True)
    chosen = jnp.take(spread, placement.T, axis=0)
    arrived = lax.all_to_all(chosen, "expert", split_axis=1, concat_axis=1, tiled=True)
    copies = arrived.shape[0]
    incoming = arrived.reshape(copies, owned, width)
    served = (serving[0].astype(jnp.float32) + incoming.astype(jnp.float32)).astype(jnp.bfloat16)
    return (
        d_hid[None],
        updated.astype(jnp.bfloat16)[None],
        first_new[None],
        squares_new[None],
        served[None],
    )


def solution(mesh):
    torus = Mesh(
        mesh.devices.reshape(4, 4, 4, mesh.shape["expert"]), ("dp_0", "dp_1", "dp_2", "expert")
    )
    return jax.shard_map(
        on_device,
        mesh=torus,
        in_specs=(
            P("expert", DP, None),
            P("expert", DP, None),
            P("expert", DP),
            P(),
            P("expert", DP, None),
            P("expert", DP, None),
            P("expert", DP, None),
            P("expert", None, DP, None),
        ),
        out_specs=(
            P("expert", DP, None),
            P("expert", DP, None),
            P("expert", DP, None),
            P("expert", DP, None),
            P("expert", None, DP, None),
        ),
        check_vma=False,
    )
```

profile of v0, /device:TPU:0, one launch (start us, length us, event | category | flops | bytes accessed | tf_op | source)
XLA Modules:
  0.0 300.9 jit_solution(9500016079672712635)
XLA Ops:
  8.0 0.0 copy-start
  8.0 0.0 reduce-scatter.8.cloned.1.call-start
  8.9 0.8 copy-done
  9.6 14.4 %multiply_bitcast_fusion = f32[1024,3584]{0,1:T(8,128)} fusion(bf16[1,1024,3584]{2,1,0:T(8,128)(2,1)} %param.9, pred[1024]{0:T(1024)(128)(4,1)S(1)} %iota_compare_fusion, bf16[1,1024,1024]{2,1,0:T(8,128)(2,1)S(1)} %copy-done), kind=kOutput, calls=%fused_computation.1 | convolution fusion | flops 7523532800 | bytes 24118272 | tf_op jit(solution)/shard_map/dot_general | solution.py:41
  24.0 0.0 reduce-scatter.8.cloned.1.call-update
  24.0 0.0 copy-start.4
  24.0 0.0 reduce-scatter.10.cloned.1.call-start
  24.1 134.3 %reduce-scatter.8.cloned.1.call-done = f32[256,3584]{0,1:T(8,128)} async-done(((f32[1024,3584]{0,1:T(8,128)}), f32[256,3584]{0,1:T(8,128)}) %reduce-scatter.8.cloned.1.call-update) | async-done | bytes 3670032 | tf_op jit(solution)/shard_map/reduce_scatter | solution.py:23
  158.4 5.2 %copy.58 = f32[256,3584]{1,0:T(8,128)} copy(f32[256,3584]{0,1:T(8,128)} %reduce-scatter.8.cloned.1.call-done) | data formatting | bytes 7340032
  163.5 0.0 reduce-scatter.10.cloned.1.call-update
  163.5 0.0 all-gather.3.cloned.1.call-start
  163.6 0.5 all-gather.3.cloned.1.call-update
  164.1 0.0 reduce-scatter.12.cloned.1.call-start
  164.2 0.0 copy-done.4
  164.2 0.1 copy.55
  164.3 0.1 reshape.51
  164.4 42.4 %reduce-scatter.10.cloned.1.call-done = f32[64,3584]{1,0:T(8,128)} async-done(((f32[256,3584]{1,0:T(8,128)}), f32[64,3584]{1,0:T(8,128)}) %reduce-scatter.10.cloned.1.call-update) | async-done | bytes 917520
  206.8 0.0 reduce-scatter.12.cloned.1.call-update
  206.9 0.0 copy-start.1
  206.9 0.0 copy-start.2
  206.9 0.0 copy-start.3
  206.9 54.5 %all-gather.3.cloned.1.call-done = bf16[1,1024,3584]{2,1,0:T(8,128)(2,1)} async-done(((bf16[1,16,3584]{2,1,0:T(8,128)(2,1)}), bf16[1,1024,3584]{2,1,0:T(8,128)(2,1)}) %all-gather.3.cloned.1.call-update) | async-done | bytes 7340048 | tf_op jit(solution)/shard_map/all_gather | solution.py:38
  261.4 13.2 %fusion.11 = bf16[1,1024,1024]{2,1,0:T(8,128)(2,1)} fusion(bf16[1,1024,3584]{2,1,0:T(8,128)(2,1)} %all-gather.3.cloned.1.call-done, bf16[1,1024,3584]{2,1,0:T(8,128)(2,1)} %param.9, pred[1024]{0:T(1024)(128)(4,1)S(1)} %iota_compare_fusion), kind=kOutput, calls=%fused_computation.13 | convolution fusion | flops 7521959936 | bytes 16778240 | tf_op jit(solution)/shard_map/dot_general | solution.py:37
  274.6 0.0 reduce-scatter.12.cloned.1.call-done
  274.6 0.0 copy-done.1
  274.6 0.0 copy-done.2
  274.6 0.0 copy-done.3
  274.6 1.9 fusion.17
  276.5 0.1 all_to_all.15
  276.5 0.5 broadcast.53
  277.0 1.4 reduce
  278.5 0.1 reshape.65
  278.6 3.8 %all_to_all.18 = bf16[2,2,14336]{2,1,0:T(2,128)(2,1)S(1)} all-to-all(bf16[2,2,14336]{2,1,0:T(2,128)(2,1)S(1)} %reshape.65), channel_id=1, replica_groups=mesh['dp_0'=4,'dp_1'=4,'dp_2'=4,'expert'=2] {'expert'}, dimensions={0} | all-to-all | bytes 229376 | tf_op jit(solution)/shard_map/all_to_all | solution.py:51
  282.4 0.1 reshape.66
  282.5 0.2 copy.65
  282.7 0.8 gather_fusion
  283.5 0.3 reshape.50
  283.8 0.6 copy_select_fusion
  284.5 4.1 %all_to_all.19 = bf16[4,2,28672]{2,0,1:T(4,128)(2,1)S(1)} all-to-all(bf16[4,2,28672]{2,0,1:T(4,128)(2,1)S(1)} %copy_select_fusion), channel_id=1, replica_groups=mesh['dp_0'=4,'dp_1'=4,'dp_2'=4,'expert'=2] {'expert'}, dimensions={1} | all-to-all | bytes 917504 | tf_op jit(solution)/shard_map/all_to_all | solution.py:53
  288.6 1.4 copy.57
  290.0 2.0 reshape.48
  291.9 1.9 add_convert_fusion
  (4 shorter events, 0.0 us)
Async XLA Ops:
  8.0 1.6 copy-start
  8.0 150.3 %reduce-scatter.8.cloned.1.call-start = ((), (), s32[]{:S(2)}) async-start(), calls=%async_computation.5 | async-start | bytes 18350080 | tf_op jit(solution)/shard_map/reduce_scatter | solution.py:23
  24.0 140.2 %copy-start.4 = (s32[2,4]{1,0:T(2,128)S(1)}, s32[2,4]{1,0:T(2,128)}, u32[]{:S(2)}) copy-start(s32[2,4]{1,0:T(2,128)} %param.11) | copy-start | bytes 100
  24.0 182.8 %reduce-scatter.10.cloned.1.call-start = ((), (), s32[]{:S(2)}) async-start(), calls=%async_computation.7 | async-start | bytes 4587520
  163.5 97.8 %all-gather.3.cloned.1.call-start = ((), (), s32[]{:S(2)}) async-start(), calls=%async_computation.6 | async-start | bytes 7454720 | tf_op jit(solution)/shard_map/all_gather | solution.py:38
  164.1 110.5 %reduce-scatter.12.cloned.1.call-start = ((), (), s32[]{:S(2)}) async-start(), calls=%async_computation.8 | async-start | bytes 1146880 | tf_op jit(solution)/shard_map/reduce_scatter | solution.py:23
  206.9 67.7 %copy-start.1 = (bf16[1,16,3584]{2,1,0:T(8,128)(2,1)S(1)}, bf16[1,16,3584]{2,1,0:T(8,128)(2,1)}, u32[]{:S(2)}) copy-start(bf16[1,16,3584]{2,1,0:T(8,128)(2,1)} %param.12) | copy-start | bytes 344068
  206.9 67.7 %copy-start.2 = (f32[1,16,3584]{2,1,0:T(8,128)S(1)}, f32[1,16,3584]{2,1,0:T(8,128)}, u32[]{:S(2)}) copy-start(f32[1,16,3584]{2,1,0:T(8,128)} %param.14) | copy-start | bytes 688132
  206.9 67.7 %copy-start.3 = (f32[1,16,3584]{2,1,0:T(8,128)S(1)}, f32[1,16,3584]{2,1,0:T(8,128)}, u32[]{:S(2)}) copy-start(f32[1,16,3584]{2,1,0:T(8,128)} %param.13) | copy-start | bytes 688132
Sparse Core Ops, SparseCore 0:
  24.1 134.1 reduce-scatter.7
  163.7 43.1 reduce-scatter.9
  209.2 22.9 reduce-scatter.11
Sparse Core Ops, SparseCore 1:
  166.8 94.5 all-gather.2
where the time goes:
time: 302 us; the launch traced here: 301 us
  waiting for transfers between devices  232 us (77%)
  matrix products  27.6 us (9%)
  between operations  16.1 us (5%)
  local copies, waits for them, and re-layouts  11.6 us (4%)
  blocking collectives  7.92 us (3%)
  other arithmetic  5.8 us (2%)
    reduce_scatter x2, waiting for transfers between devices, summed_rows(): nearer = lax.psum_scatter(array, axes[0], scatter_dimension=dim, tiled=True)  134 us
    all_gather x1, waiting for transfers between devices, on_device(): lax.all_gather(matrix, DP, axis=0, tiled=True)  54.5 us
    unnamed x5, waiting for transfers between devices  43 us
    dot_general x1, matrix products, on_device(): jnp.dot(acts.T, masked, preferred_element_type=jnp.float32)  14.4 us
    dot_general x1, matrix products, on_device(): jnp.dot(masked, lax.all_gather(matrix, DP, axis=0, tiled=True).T, preferr...  13.2 us
    unnamed x14, local copies, waits for them, and re-layouts  6.33 us
  transfers between devices with their start and end apart: 4, of which 3 were waited for; matrix products, arithmetic and copies ran while one was open for 4% of the time, Pallas kernels for 0%

commit v1 on v0

v1 whole, which is shorter than its diff:
```python
import functools

import jax
import jax.numpy as jnp
from jax import lax
from jax.experimental import pallas as pl
from jax.experimental.pallas import tpu as pltpu
from jax.sharding import Mesh
from jax.sharding import PartitionSpec as P

DP = ("dp_0", "dp_1", "dp_2")
MESH = pl.DeviceIdType.MESH
RING = 4

beta_one = 0.9
beta_two = 0.95
bias_one = 1.0 - 0.9**20
bias_two = 1.0 - 0.95**20
learn_rate = 0.05
decay_rate = 0.1
epsilon = 1e-08

TILE = 256
TOP = 32767.0
LANES = 3
GATHER = ((2, 1, 0), (0, 2, 1), (1, 0, 2))
SCATTER = ((0, 1, 2), (1, 2, 0), (2, 0, 1))


def lane_columns(width):
    tiles = width // TILE
    low = tiles // LANES
    counts = [low + (1 if lane < tiles - low * LANES else 0) for lane in range(LANES)]
    starts = [sum(counts[:lane]) * TILE for lane in range(LANES)]
    return tuple((start, count * TILE) for start, count in zip(starts, counts))


def fused(
    scale, lanes,
    counts, placement, hid_in, cot_in, w_in, mom_in, sec_in, srv_in,
    dh_out, nw_out, nm_out, ns_out, so_out,
    weights, hid, hid_t, cot, grads, mom, sec, srv, nw, nm, ns, so, delta,
    sent1, got1, sent2, got2, sent3, got3,
    sent1_top, got1_top, sent2_top, got2_top, sent3_top, got3_top,
    ga_send, ga_recv, gb_send, gb_recv, gc_send, gc_recv,
    r1_send, r1_recv, r1t_send, r1t_recv,
    r2_send, r2_recv, r2t_send, r2t_recv,
    r3_send, r3_recv, r3t_send, r3t_recv,
    d_send, d_recv, in_sem, dh_sem, out_sem,
):
    me = tuple(lax.axis_index(name) for name in DP)
    core = lax.axis_index("expert")
    tokens = hid.shape[0]
    owned = weights.shape[3]

    def on_ring(axis, offset):
        return lax.rem(me[axis] + (offset + RING) % RING, RING)

    def remote(src, dst, send, recv, axis, offset):
        return pltpu.make_async_remote_copy(
            src_ref=src, dst_ref=dst, send_sem=send, recv_sem=recv,
            device_id={DP[axis]: on_ring(axis, offset)}, device_id_type=MESH,
        )

    def block(ref, at, columns=None):
        index = tuple(at.get(axis, slice(None)) for axis in range(3))
        if columns is None:
            return ref.at[index]
        return ref.at[index + (slice(None), pl.ds(*columns))]

    load_w = pltpu.make_async_copy(w_in, weights.at[me[0], me[1], me[2]], in_sem.at[0])
    load_hid = pltpu.make_async_copy(hid_in, hid, in_sem.at[1])
    load_cot = pltpu.make_async_copy(cot_in, cot, in_sem.at[2])
    load_mom = pltpu.make_async_copy(mom_in, mom, in_sem.at[3])
    load_sec = pltpu.make_async_copy(sec_in, sec, in_sem.at[4])
    load_srv = pltpu.make_async_copy(srv_in, srv, in_sem.at[5])
    for load in (load_w, load_hid, load_cot, load_mom, load_sec, load_srv):
        load.start()

    barrier = pltpu.get_barrier_semaphore()
    for axis in range(3):
        for offset in range(1, RING):
            pl.semaphore_signal(
                barrier, inc=1, device_id={DP[axis]: on_ring(axis, offset)}, device_id_type=MESH
            )
    pl.semaphore_signal(barrier, inc=1, device_id={"expert": 1 - core}, device_id_type=MESH)
    pl.semaphore_wait(barrier, 3 * (RING - 1) + 1)

    started = []

    def start(copy):
        copy.start()
        started.append(copy)
        return copy

    def gather_small(stage, send, recv):
        copies = [[] for _ in range(LANES)]
        for offset in (1, 3, 2):
            for lane in range(LANES):
                order = GATHER[lane]
                axis = order[stage]
                at = {other: me[other] for other in order[stage:]}
                part = block(weights, at, lanes[lane])
                copies[lane].append(
                    start(remote(part, part, send.at[lane, offset - 1], recv.at[lane, offset - 1], axis, offset))
                )
        return copies

    def arrive(copies):
        for lane in copies:
            for copy in lane:
                copy.wait_recv()

    def half(order_axis, which):
        return {order_axis: pl.ds(2 * which, 2)}

    def gather_large_first():
        copies = []
        for lane in range(LANES):
            mid, axis = GATHER[lane][1], GATHER[lane][2]
            row = []
            for slot, (offset, which) in enumerate(((1, 0), (3, 1), (1, 1), (3, 0))):
                part = block(weights, {axis: me[axis], **half(mid, which)}, lanes[lane])
                row.append(start(remote(part, part, gc_send.at[lane, slot], gc_recv.at[lane, slot], axis, offset)))
            copies.append(row)
        return copies

    def gather_large_second(first):
        copies = []
        for lane in range(LANES):
            mid, axis = GATHER[lane][1], GATHER[lane][2]
            row = []
            for slot, (offset, which) in enumerate(((1, 0), (3, 1))):
                first[lane][slot].wait_recv()
                part = block(weights, {axis: on_ring(axis, -offset), **half(mid, which)}, lanes[lane])
                row.append(start(remote(part, part, gc_send.at[lane, 4 + slot], gc_recv.at[lane, 4 + slot], axis, offset)))
            copies.append(row)
        return copies

    load_w.wait()
    first = gather_small(0, ga_send, ga_recv)

    load_hid.wait()
    limit = counts[0, 0]

    def turn(step):
        rows = pl.ds(pl.multiple_of(step * TILE, TILE), TILE)
        slots = lax.broadcasted_iota(jnp.int32, (TILE, 1), 0) + step * TILE
        piece = jnp.where(slots < limit, hid[rows, :].astype(jnp.float32), 0.0)
        hid_t[:, rows] = piece.T.astype(hid_t.dtype)

    def tiles(count, body):
        def step(at, carry):
            body(at)
            return carry
        lax.fori_loop(0, count, step, 0)

    tiles(tokens // TILE // 2, turn)
    arrive(first)
    second = gather_small(1, gb_send, gb_recv)
    tiles(tokens // TILE - tokens // TILE // 2, lambda at: turn(at + tokens // TILE // 2))

    def product(lane, low, high):
        begin = lanes[lane][0]

        def body(at):
            columns = pl.ds(pl.multiple_of(begin + (low + at) * TILE, TILE), TILE)
            value = jnp.dot(hid_t[...], cot[:, columns], preferred_element_type=jnp.float32)
            grads[:, :, :, :, columns] = value.reshape(RING, RING, RING, owned, TILE)
        tiles(high - low, body)

    def encode(read, count, write, top_ref):
        def largest(at, top):
            return jnp.maximum(top, jnp.abs(read(at)))
        shape = read(0).shape
        top = lax.fori_loop(0, count, largest, jnp.zeros(shape, jnp.float32))
        top = jnp.maximum(jnp.max(top, keepdims=True), 1e-30)
        factor = TOP / top

        def code(at):
            write(at, jnp.round(read(at) * factor).astype(jnp.int32).astype(jnp.int16))
        tiles(count, code)
        top_ref[...] = jnp.broadcast_to(top * (1.0 / TOP), top_ref.shape)

    def three(order, first_at, second_at, third_at):
        at = {order[0]: first_at, order[1]: second_at, order[2]: third_at}
        return at[0], at[1], at[2]

    MESSAGES = ((2, 0, 1), (1, 1, 1), (1, 0, 1), (2, 1, 3), (3, 0, 3), (3, 1, 3))

    def scatter_large(lane, message, forwarded):
        order = SCATTER[lane]
        begin, width = lanes[lane]
        owner, which, way = MESSAGES[message]
        row = on_ring(order[0], owner)

        def read(at):
            z, y, x = three(order, row, 2 * which + at // RING, at % RING)
            value = grads[z, y, x, :, pl.ds(begin, width)]
            if forwarded is not None:
                value += decoded(got1.at[lane, forwarded], got1_top.at[lane, forwarded], lane, at)
            return value

        def write(at, value):
            sent1[lane, message, at, :, pl.ds(0, width)] = value

        if forwarded is not None:
            def add(at):
                z, y, x = three(order, row, 2 * which + at // RING, at % RING)
                grads[z, y, x, :, pl.ds(begin, width)] = read(at)
            tiles(2 * RING, add)
            encode(lambda at: grads[three(order, row, 2 * which + at // RING, at % RING) + (slice(None), pl.ds(begin, width))],
                   2 * RING, write, sent1_top.at[lane, message])
        else:
            encode(read, 2 * RING, write, sent1_top.at[lane, message])
        columns = pl.ds(0, width)
        return (
            start(remote(sent1_top.at[lane, message], got1_top.at[lane, message],
                         r1t_send.at[lane, message], r1t_recv.at[lane, message], order[0], way)),
            start(remote(sent1.at[lane, message, :, :, columns], got1.at[lane, message, :, :, columns],
                         r1_send.at[lane, message], r1_recv.at[lane, message], order[0], way)),
        )

    def decoded(codes, top_ref, lane, at):
        width = lanes[lane][1]
        return codes[at, :, pl.ds(0, width)].astype(jnp.float32) * top_ref[0:1, 0:1]

    def landed(pair):
        pair[0].wait_recv()
        pair[1].wait_recv()

    tile_count = [width // TILE for _, width in lanes]
    large = [dict() for _ in range(LANES)]

    load_cot.wait()
    product(0, 0, 2)
    arrive(second)
    third = gather_large_first()
    product(0, 2, tile_count[0])
    for message in (0, 3):
        large[0][message] = scatter_large(0, message, None)
    product(1, 0, tile_count[1])
    for message in (0, 3):
        large[1][message] = scatter_large(1, message, None)
    product(2, 0, tile_count[2])
    for message in (0, 3):
        large[2][message] = scatter_large(2, message, None)
    fourth = gather_large_second(third)
    for lane in range(LANES):
        for message in (1, 4):
            large[lane][message] = scatter_large(lane, message, None)

    limit_mask = lax.broadcasted_iota(jnp.int32, (tokens, 1), 0) < limit
    quarter = RING * RING * owned

    def d_hidden(at):
        rows = weights[at].reshape(quarter, weights.shape[4])
        value = lax.dot_general(
            cot[...], rows, (((1,), (1,)), ((), ())), preferred_element_type=jnp.float32
        )
        value = jnp.where(limit_mask, scale * value, 0.0)
        hid[:, pl.ds(pl.multiple_of(at * quarter, quarter), quarter)] = value.astype(hid.dtype)

    for lane in range(LANES):
        for slot in (2, 3):
            third[lane][slot].wait_recv()
    arrive(fourth)
    tiles(2, d_hidden)

    for lane in range(LANES):
        landed(large[lane][0])
        large[lane][2] = scatter_large(lane, 2, 0)
        landed(large[lane][3])
        large[lane][5] = scatter_large(lane, 5, 3)

    tiles(2, lambda at: d_hidden(at + 2))
    store_dh = pltpu.make_async_copy(hid, dh_out, dh_sem.at[0])
    store_dh.start()

    medium = [[] for _ in range(LANES)]
    for lane in range(LANES):
        order = SCATTER[lane]
        begin, width = lanes[lane]
        for message in (1, 4, 2, 5):
            landed(large[lane][message])

        for which, (near, far) in enumerate(((4, 2), (1, 5))):
            def add(at, which=which, near=near, far=far):
                z, y, x = three(order, me[order[0]], 2 * which + at // RING, at % RING)
                grads[z, y, x, :, pl.ds(begin, width)] = (
                    grads[z, y, x, :, pl.ds(begin, width)]
                    + decoded(got1.at[lane, near], got1_top.at[lane, near], lane, at)
                    + decoded(got1.at[lane, far], got1_top.at[lane, far], lane, at)
                )
            tiles(2 * RING, add)
        for offset in (2, 1, 3):
            slot = offset - 1

            def read(at):
                z, y, x = three(order, me[order[0]], on_ring(order[1], offset), at)
                return grads[z, y, x, :, pl.ds(begin, width)]

            def write(at, value):
                sent2[lane, slot, at, :, pl.ds(0, width)] = value
            encode(read, RING, write, sent2_top.at[lane, slot])
            columns = pl.ds(0, width)
            medium[lane].append((
                start(remote(sent2_top.at[lane, slot], got2_top.at[lane, slot],
                             r2t_send.at[lane, slot], r2t_recv.at[lane, slot], order[1], offset)),
                start(remote(sent2.at[lane, slot, :, :, columns], got2.at[lane, slot, :, :, columns],
                             r2_send.at[lane, slot], r2_recv.at[lane, slot], order[1], offset)),
            ))

    small = [[] for _ in range(LANES)]
    for lane in range(LANES):
        order = SCATTER[lane]
        begin, width = lanes[lane]
        for pair in medium[lane]:
            landed(pair)

        def add(at):
            z, y, x = three(order, me[order[0]], me[order[1]], at)
            value = grads[z, y, x, :, pl.ds(begin, width)]
            for slot in range(RING - 1):
                value += decoded(got2.at[lane, slot], got2_top.at[lane, slot], lane, at)
            grads[z, y, x, :, pl.ds(begin, width)] = value
        tiles(RING, add)
        for offset in (2, 1, 3):
            slot = offset - 1

            def read(at):
                z, y, x = three(order, me[order[0]], me[order[1]], on_ring(order[2], offset))
                return grads[z, y, x, :, pl.ds(begin, width)]

            def write(at, value):
                sent3[lane, slot, at, :, pl.ds(0, width)] = value
            encode(read, 1, write, sent3_top.at[lane, slot])
            columns = pl.ds(0, width)
            small[lane].append((
                start(remote(sent3_top.at[lane, slot], got3_top.at[lane, slot],
                             r3t_send.at[lane, slot], r3t_recv.at[lane, slot], order[2], offset)),
                start(remote(sent3.at[lane, slot, :, :, columns], got3.at[lane, slot, :, :, columns],
                             r3_send.at[lane, slot], r3_recv.at[lane, slot], order[2], offset)),
            ))

    for load in (load_mom, load_sec, load_srv):
        load.wait()
    shared = []
    stores = []
    for lane in range(LANES):
        begin, width = lanes[lane]
        columns = pl.ds(begin, width)
        for pair in small[lane]:
            landed(pair)
        total = grads[me[0], me[1], me[2], :, columns]
        for slot in range(RING - 1):
            total += decoded(got3.at[lane, slot], got3_top.at[lane, slot], lane, 0)
        grad = scale * total
        first_new = beta_one * mom[:, columns] + (1.0 - beta_one) * grad
        squares_new = beta_two * sec[:, columns] + (1.0 - beta_two) * grad * grad
        step = first_new / bias_one / (jnp.sqrt(squares_new / bias_two) + epsilon)
        current = weights[me[0], me[1], me[2], :, columns].astype(jnp.float32)
        updated = current - learn_rate * (step + decay_rate * current)
        delta[core, :, columns] = (updated - current).astype(delta.dtype)
        part = delta.at[core, :, columns]
        shared.append(start(pltpu.make_async_remote_copy(
            src_ref=part, dst_ref=part, send_sem=d_send.at[lane], recv_sem=d_recv.at[lane],
            device_id={"expert": 1 - core}, device_id_type=MESH,
        )))
        nw[:, columns] = updated.astype(nw.dtype)
        nm[:, columns] = first_new
        ns[:, columns] = squares_new
        for slot, (src, dst) in enumerate(((nw, nw_out), (nm, nm_out), (ns, ns_out))):
            store = pltpu.make_async_copy(src.at[:, columns], dst.at[:, columns], out_sem.at[lane, slot])
            store.start()
            stores.append(store)
    for lane in range(LANES):
        begin, width = lanes[lane]
        columns = pl.ds(begin, width)
        shared[lane].wait_recv()
        choices = [delta[expert, :, columns].astype(jnp.float32) for expert in range(2)]
        for replica in range(srv.shape[0]):
            pick = jnp.full((owned, width), placement[core, replica], jnp.int32) == 0
            incoming = jnp.where(pick, choices[0], choices[1])
            so[replica, :, columns] = (srv[replica, :, columns].astype(jnp.float32) + incoming).astype(so.dtype)
        store = pltpu.make_async_copy(so.at[:, :, columns], so_out.at[:, :, columns], out_sem.at[lane, 3])
        store.start()
        stores.append(store)
    for copy in started:
        copy.wait_send()
    for store in stores:
        store.wait()
    store_dh.wait()


def on_device(hidden, cotangent, counts, placement, weight, moment, second, serving):
    tokens, rows = hidden.shape[1:]
    width = cotangent.shape[2]
    owned = weight.shape[1]
    copies = serving.shape[1]
    lanes = lane_columns(width)
    widest = max(count for _, count in lanes)
    scale = width ** (-0.5)
    anywhere = pl.BlockSpec(memory_space=pl.ANY)
    scalars = pl.BlockSpec(memory_space=pltpu.SMEM)
    f32, bf16, i16 = jnp.float32, jnp.bfloat16, jnp.int16
    dma = pltpu.SemaphoreType.DMA
    outs = pl.pallas_call(
        functools.partial(fused, scale, lanes),
        out_shape=(
            jax.ShapeDtypeStruct((tokens, rows), bf16),
            jax.ShapeDtypeStruct((owned, width), bf16),
            jax.ShapeDtypeStruct((owned, width), f32),
            jax.ShapeDtypeStruct((owned, width), f32),
            jax.ShapeDtypeStruct((copies, owned, width), bf16),
        ),
        in_specs=[scalars, scalars] + [anywhere] * 6,
        out_specs=[anywhere] * 5,
        scratch_shapes=[
            pltpu.VMEM((RING, RING, RING, owned, width), bf16),
            pltpu.VMEM((tokens, rows), bf16),
            pltpu.VMEM((rows, tokens), bf16),
            pltpu.VMEM((tokens, width), bf16),
            pltpu.VMEM((RING, RING, RING, owned, width), f32),
            pltpu.VMEM((owned, width), f32),
            pltpu.VMEM((owned, width), f32),
            pltpu.VMEM((copies, owned, width), bf16),
            pltpu.VMEM((owned, width), bf16),
            pltpu.VMEM((owned, width), f32),
            pltpu.VMEM((owned, width), f32),
            pltpu.VMEM((copies, owned, width), bf16),
            pltpu.VMEM((2, owned, width), bf16),
            pltpu.VMEM((LANES, 6, 2 * RING, owned, widest), i16),
            pltpu.VMEM((LANES, 6, 2 * RING, owned, widest), i16),
            pltpu.VMEM((LANES, 3, RING, owned, widest), i16),
            pltpu.VMEM((LANES, 3, RING, owned, widest), i16),
            pltpu.VMEM((LANES, 3, 1, owned, widest), i16),
            pltpu.VMEM((LANES, 3, 1, owned, widest), i16),
            pltpu.VMEM((LANES, 6, 8, 128), f32),
            pltpu.VMEM((LANES, 6, 8, 128), f32),
            pltpu.VMEM((LANES, 3, 8, 128), f32),
            pltpu.VMEM((LANES, 3, 8, 128), f32),
            pltpu.VMEM((LANES, 3, 8, 128), f32),
            pltpu.VMEM((LANES, 3, 8, 128), f32),
        ]
        + [dma((LANES, 3))] * 4
        + [dma((LANES, 6))] * 2
        + [dma((LANES, 6))] * 4
        + [dma((LANES, 3))] * 8
        + [dma((LANES,))] * 2
        + [dma((6,)), dma((1,)), dma((LANES, 4))],
        compiler_params=pltpu.CompilerParams(
            collective_id=0, has_side_effects=True, vmem_limit_bytes=62 * 2**20
        ),
        cost_estimate=pl.CostEstimate(flops=4 * tokens * rows * width, bytes_accessed=2**25, transcendentals=0),
    )(counts, placement, hidden[0], cotangent[0], weight[0], moment[0], second[0], serving[0])
    return tuple(out[None] for out in outs)


def solution(mesh):
    torus = Mesh(
        mesh.devices.reshape(RING, RING, RING, mesh.shape["expert"]), ("dp_0", "dp_1", "dp_2", "expert")
    )
    return jax.shard_map(
        on_device,
        mesh=torus,
        in_specs=(
            P("expert", DP, None),
            P("expert", DP, None),
            P("expert", DP),
            P(),
            P("expert", DP, None),
            P("expert", DP, None),
            P("expert", DP, None),
            P("expert", None, DP, None),
        ),
        out_specs=(
            P("expert", DP, None),
            P("expert", DP, None),
            P("expert", DP, None),
            P("expert", DP, None),
            P("expert", None, DP, None),
        ),
        check_vma=False,
    )
```

time: 302 us -> 94.6 us (0.31)
  the two profiles are of different devices: /device:TPU:0 before, /device:TPU:33 now
where the time goes in v1:
time: 94.6 us; the launch traced here: 94.4 us
  Pallas kernels  87.1 us (92%)
  local copies, waits for them, and re-layouts  5.97 us (6%)
  between operations  1.32 us (1%)
    pallas_call x1, Pallas kernels, on_device(): pl.pallas_call(functools.partial(fused, scale, lanes), out_shape=(jax.Sha...  87.1 us
    unnamed x13, local copies, waits for them, and re-layouts  5.97 us

profile of v1, /device:TPU:33, one launch (start us, length us, event | category | flops | bytes accessed | tf_op | source)
XLA Modules:
  0.0 94.4 jit_solution(8227223155605053171)
XLA Ops:
  1.3 87.1 %shard_map.119 = (bf16[1024,1024]{1,0:T(8,128)(2,1)}, bf16[16,3584]{1,0:T(8,128)(2,1)}, f32[16,3584]{1,0:T(8,128)}, f32[16,3584]{1,0:T(8,128)}, bf16[4,16,3584]{2,1,0:T(8,128)(2,1)}) custom-call(s32[1,1]{1,0:T(1,128)S(6)} %copy.18.counts, s32[2,4]{1,0:T(2,128)} %placement.1, bf16[1024,1024]{1,0:T(8,128)(2,1)} %bitcast.17, bf16[1024,3584]{1,0:T(8,128)(2,1)} %bitcast.16, ...), custom_call_target="tpu_custom_call" | custom-call | flops 15032385536 | bytes 33554432 | tf_op jit(solution)/shard_map/pallas_call | solution.py:408
  88.4 0.0 copy-start.3
  88.4 0.0 copy-start.2
  88.4 0.0 copy-start.1
  88.4 0.0 copy-start
  88.4 3.2 %copy.19 = bf16[1,1024,1024]{2,1,0:T(8,128)(2,1)} copy(bf16[1,1024,1024]{2,1,0:T(8,128)(2,1)} %bitcast.11) | data formatting | bytes 4194304
  91.6 0.0 copy-done.3
  91.6 0.6 copy.20
  92.2 0.0 copy-done.2
  92.2 0.7 copy.21
  92.9 0.0 copy-done.1
  92.9 0.7 copy.22
  93.6 0.0 copy-done
  93.6 0.8 copy.23
Async XLA Ops:
  88.4 3.2 %copy-start.3 = (bf16[16,3584]{1,0:T(8,128)(2,1)S(1)}, bf16[16,3584]{1,0:T(8,128)(2,1)}, u32[]{:S(2)}) copy-start(bf16[16,3584]{1,0:T(8,128)(2,1)} %get-tuple-element.11) | copy-start | bytes 344068
  88.4 3.8 %copy-start.2 = (f32[16,3584]{1,0:T(8,128)S(1)}, f32[16,3584]{1,0:T(8,128)}, u32[]{:S(2)}) copy-start(f32[16,3584]{1,0:T(8,128)} %get-tuple-element.12) | copy-start | bytes 688132
  88.4 4.5 %copy-start.1 = (f32[16,3584]{1,0:T(8,128)S(1)}, f32[16,3584]{1,0:T(8,128)}, u32[]{:S(2)}) copy-start(f32[16,3584]{1,0:T(8,128)} %get-tuple-element.13) | copy-start | bytes 688132
  88.4 5.2 %copy-start = (bf16[4,16,3584]{2,1,0:T(8,128)(2,1)S(1)}, bf16[4,16,3584]{2,1,0:T(8,128)(2,1)}, u32[]{:S(2)}) copy-start(bf16[4,16,3584]{2,1,0:T(8,128)(2,1)} %get-tuple-element.14) | copy-start | bytes 1376260

commit v2 on v0

v2 whole, which is shorter than its diff:
```python
import functools

import jax
import jax.numpy as jnp
from jax import lax
from jax.experimental import pallas as pl
from jax.experimental.pallas import tpu as pltpu
from jax.sharding import Mesh
from jax.sharding import PartitionSpec as P

DP = ("dp_0", "dp_1", "dp_2")
MESH = pl.DeviceIdType.MESH
RING = 4

beta_one = 0.9
beta_two = 0.95
bias_one = 1.0 - 0.9**20
bias_two = 1.0 - 0.95**20
learn_rate = 0.05
decay_rate = 0.1
epsilon = 1e-08

TILE = 256
TOP = 32767.0
LANES = 3
GATHER = ((2, 1, 0), (0, 2, 1), (1, 0, 2))
SCATTER = ((0, 1, 2), (1, 2, 0), (2, 0, 1))


def lane_columns(width, wider):
    tiles = width // 128
    low = tiles // LANES
    counts = [low] * LANES
    for at in range(tiles - low * LANES):
        counts[(wider + at) % LANES] += 1
    starts = [sum(counts[:lane]) * 128 for lane in range(LANES)]
    return tuple((start, count * 128) for start, count in zip(starts, counts))


def fused(
    scale, gather_lanes, lanes,
    counts, placement, hid_in, cot_in, w_in, mom_in, sec_in, srv_in,
    dh, nw, nm, ns, so,
    weights, hid, hid_t, cot, grads, mom, sec, srv, delta,
    sent1, got1, sent2, got2, sent3, got3,
    sent1_top, got1_top, sent2_top, got2_top, sent3_top, got3_top,
    ga_send, ga_recv, gb_send, gb_recv, gc_send, gc_recv,
    r1_send, r1_recv, r1t_send, r1t_recv,
    r2_send, r2_recv, r2t_send, r2t_recv,
    r3_send, r3_recv, r3t_send, r3t_recv,
    d_send, d_recv, in_sem,
):
    me = tuple(lax.axis_index(name) for name in DP)
    core = lax.axis_index("expert")
    tokens = hid.shape[0]
    owned = weights.shape[3]

    def on_ring(axis, offset):
        return lax.rem(me[axis] + (offset + RING) % RING, RING)

    def remote(src, dst, send, recv, axis, offset):
        return pltpu.make_async_remote_copy(
            src_ref=src, dst_ref=dst, send_sem=send, recv_sem=recv,
            device_id={DP[axis]: on_ring(axis, offset)}, device_id_type=MESH,
        )

    def block(at, columns):
        index = tuple(at.get(axis, slice(None)) for axis in range(3))
        return weights.at[index + (slice(None), pl.ds(*columns))]

    load_w = pltpu.make_async_copy(w_in, weights.at[me[0], me[1], me[2]], in_sem.at[0])
    load_hid = pltpu.make_async_copy(hid_in, hid, in_sem.at[1])
    load_cot = pltpu.make_async_copy(cot_in, cot, in_sem.at[2])
    load_mom = pltpu.make_async_copy(mom_in, mom, in_sem.at[3])
    load_sec = pltpu.make_async_copy(sec_in, sec, in_sem.at[4])
    load_srv = pltpu.make_async_copy(srv_in, srv, in_sem.at[5])
    for load in (load_w, load_hid, load_cot, load_mom, load_sec, load_srv):
        load.start()

    barrier = pltpu.get_barrier_semaphore()
    for axis in range(3):
        for offset in range(1, RING):
            pl.semaphore_signal(
                barrier, inc=1, device_id={DP[axis]: on_ring(axis, offset)}, device_id_type=MESH
            )
    pl.semaphore_signal(barrier, inc=1, device_id={"expert": 1 - core}, device_id_type=MESH)
    pl.semaphore_wait(barrier, 3 * (RING - 1) + 1)

    def tiles(count, body):
        def step(at, carry):
            body(at)
            return carry
        lax.fori_loop(0, count, step, 0)

    def part_of(step):
        return jnp.where(step == 0, 2, jnp.where(step == 1, 1, jnp.where(step == 2, 3, 0)))

    def way_of(k):
        return 1 + 2 * lax.rem(k, 2)

    def gather_small(lane, stage, offset, send, recv):
        order = GATHER[lane]
        part = block({axis: me[axis] for axis in order[stage:]}, gather_lanes[lane])
        return remote(part, part, send.at[lane, offset - 1], recv.at[lane, offset - 1], order[stage], offset)

    def gather_large(lane, k, slot):
        _, mid, axis = GATHER[lane]
        way = way_of(k)
        holder = on_ring(axis, -way) if slot == 2 else me[axis]
        part = block({mid: on_ring(mid, k), axis: holder}, gather_lanes[lane])
        offset = RING - way if slot == 1 else way
        return remote(part, part, gc_send.at[lane, k, slot], gc_recv.at[lane, k, slot], axis, offset)

    limit = counts[0, 0]

    def turn(step):
        rows = pl.ds(pl.multiple_of(step * TILE, TILE), TILE)
        slots = lax.broadcasted_iota(jnp.int32, (TILE, 1), 0) + step * TILE
        piece = jnp.where(slots < limit, hid[rows, :].astype(jnp.float32), 0.0)
        hid_t[:, rows] = piece.T.astype(hid_t.dtype)

    def product(at):
        columns = pl.ds(pl.multiple_of(at * TILE, TILE), TILE)
        value = jnp.dot(hid_t[...], cot[:, columns], preferred_element_type=jnp.float32)
        grads[:, :, :, :, columns] = value.reshape(RING, RING, RING, owned, TILE)

    def place(order, first_at, second_at, third_at):
        at = {order[0]: first_at, order[1]: second_at, order[2]: third_at}
        return at[0], at[1], at[2]

    def spread(tile, width):
        rows = jnp.concatenate([tile] * (owned // 8), axis=0)
        return jnp.concatenate([rows] * (width // 128), axis=1)

    def decoded(codes, top_ref, lane, at):
        width = lanes[lane][1]
        return codes[at, :, pl.ds(0, width)].astype(jnp.float32) * spread(top_ref[...], width)

    def encode(lane, where, count, parts, codes, top_ref):
        begin, width = lanes[lane]
        columns = pl.ds(begin, width)

        def largest(at, top):
            index = where(at) + (slice(None), columns)
            value = grads[index]
            for part in parts:
                value += decoded(part[0], part[1], lane, at)
            if parts:
                grads[index] = value
            return jnp.maximum(top, jnp.abs(value))
        top = lax.fori_loop(0, count, largest, jnp.zeros((owned, width), jnp.float32))
        top = largest_piece(top)
        factor = TOP / top
        top_ref[...] = top * (1.0 / TOP)

        def code(at):
            value = grads[where(at) + (slice(None), columns)]
            codes[at, :, pl.ds(0, width)] = jnp.round(value * spread(factor, width)).astype(jnp.int32).astype(jnp.int16)
        tiles(count, code)

    def code_copies(lane, slot, buffers, sems, axis, offset):
        sent, sent_top, got, got_top = buffers
        columns = pl.ds(0, lanes[lane][1])
        return (
            remote(sent_top.at[slot], got_top.at[slot], sems[2].at[slot], sems[3].at[slot], axis, offset),
            remote(sent.at[slot + (slice(None), slice(None), columns)],
                   got.at[slot + (slice(None), slice(None), columns)],
                   sems[0].at[slot], sems[1].at[slot], axis, offset),
        )

    def begin_all(pair):
        for copy in pair:
            copy.start()

    def landed(pair):
        for copy in pair:
            copy.wait_recv()

    def gone(pair):
        for copy in pair:
            copy.wait_send()

    buffers1 = (sent1, sent1_top, got1, got1_top)
    buffers2 = (sent2, sent2_top, got2, got2_top)
    buffers3 = (sent3, sent3_top, got3, got3_top)
    sems1 = (r1_send, r1_recv, r1t_send, r1t_recv)
    sems2 = (r2_send, r2_recv, r2t_send, r2t_recv)
    sems3 = (r3_send, r3_recv, r3t_send, r3t_recv)

    def large(lane, k, message):
        way = way_of(k)
        return code_copies(lane, (lane, k, message), buffers1, sems1, SCATTER[lane][0],
                           RING - way if message == 1 else way)

    def medium(lane, k):
        return code_copies(lane, (lane, k - 1), buffers2, sems2, SCATTER[lane][1], k)

    def small(lane, k):
        return code_copies(lane, (lane, k - 1), buffers3, sems3, SCATTER[lane][2], k)

    def scatter_large(lane, k, message):
        order = SCATTER[lane]
        way = way_of(k)
        row = on_ring(order[0], (2, RING - way, way)[message])
        middle = on_ring(order[1], k)
        parts = []
        if message == 2:
            landed(large(lane, k, 0))
            parts = [(got1.at[lane, k, 0], got1_top.at[lane, k, 0])]
        encode(lane, lambda at: place(order, row, middle, at), RING, parts,
               sent1.at[lane, k, message], sent1_top.at[lane, k, message])
        begin_all(large(lane, k, message))

    def near_parts(lane, k):
        for message in (1, 2):
            landed(large(lane, k, message))
        return [(got1.at[lane, k, message], got1_top.at[lane, k, message]) for message in (1, 2)]

    def scatter_middle(lane, k):
        order = SCATTER[lane]
        middle = on_ring(order[1], k)
        encode(lane, lambda at: place(order, me[order[0]], middle, at), RING, near_parts(lane, k),
               sent2.at[lane, k - 1], sent2_top.at[lane, k - 1])
        begin_all(medium(lane, k))

    def own_parts(lane):
        parts = near_parts(lane, 0)
        for k in range(1, RING):
            landed(medium(lane, k))
            parts.append((got2.at[lane, k - 1], got2_top.at[lane, k - 1]))
        return parts

    def own_value(lane, parts, at):
        order = SCATTER[lane]
        value = grads[place(order, me[order[0]], me[order[1]], at) + (slice(None), pl.ds(*lanes[lane]))]
        for part in parts:
            value += decoded(part[0], part[1], lane, at)
        return value

    def largest_piece(top):
        pieces = [top[row : row + 8, column : column + 128]
                  for row in range(0, top.shape[0], 8) for column in range(0, top.shape[1], 128)]
        while len(pieces) > 1:
            pieces = [jnp.maximum(*pieces[at : at + 2]) if at + 1 < len(pieces) else pieces[at]
                      for at in range(0, len(pieces), 2)]
        return jnp.maximum(pieces[0], 1e-30)

    def scatter_small(lane, k, parts):
        width = lanes[lane][1]
        value = own_value(lane, parts, on_ring(SCATTER[lane][2], k))
        top = largest_piece(jnp.abs(value))
        sent3_top[lane, k - 1] = top * (1.0 / TOP)
        sent3[lane, k - 1, 0, :, pl.ds(0, width)] = (
            jnp.round(value * spread(TOP / top, width)).astype(jnp.int32).astype(jnp.int16)
        )
        begin_all(small(lane, k))

    limit_mask = lax.broadcasted_iota(jnp.int32, (tokens, 1), 0) < limit
    quarter = RING * RING * owned

    def d_hidden(at):
        rows = weights[at].reshape(quarter, weights.shape[4])
        value = lax.dot_general(
            cot[...], rows, (((1,), (1,)), ((), ())), preferred_element_type=jnp.float32
        )
        value = jnp.where(limit_mask, scale * value, 0.0)
        dh[:, pl.ds(pl.multiple_of(at * quarter, quarter), quarter)] = value.astype(dh.dtype)

    every = range(LANES)

    load_w.wait()
    for offset in (1, 3, 2):
        for lane in every:
            gather_small(lane, 0, offset, ga_send, ga_recv).start()
    load_hid.wait()
    tiles(tokens // TILE, turn)
    for offset in (1, 3, 2):
        for lane in every:
            gather_small(lane, 0, offset, ga_send, ga_recv).wait_recv()
    for offset in (1, 3, 2):
        for lane in every:
            gather_small(lane, 1, offset, gb_send, gb_recv).start()
    for slot in range(2):
        for lane in every:
            gather_large(lane, 0, slot).start()
    load_cot.wait()
    tiles(cot.shape[1] // TILE, product)
    for offset in (3, 1, 2):
        for lane in every:
            gather_small(lane, 1, offset, gb_send, gb_recv).wait_recv()
        for slot in range(2):
            for lane in every:
                gather_large(lane, RING - offset, slot).start()

    def near_and_far(step):
        k = part_of(step)
        for lane in every:
            scatter_large(lane, k, 0)
            scatter_large(lane, k, 1)
    tiles(RING, near_and_far)

    def onward(step):
        k = part_of(step)
        for lane in every:
            gather_large(lane, lax.rem(k + 2, RING), 0).wait_recv()
            gather_large(lane, lax.rem(k + 2, RING), 2).start()
        for lane in every:
            scatter_large(lane, k, 2)
    tiles(RING, onward)

    def gathered(k):
        for lane in every:
            gather_large(lane, k, 1).wait_recv()
            gather_large(lane, k, 2).wait_recv()
    tiles(RING, gathered)

    def second_half(step):
        d_hidden(step)

        @pl.when(step < RING - 1)
        def _():
            k = part_of(step)
            for lane in every:
                scatter_middle(lane, k)
    tiles(RING, second_half)
    for lane in every:
        parts = own_parts(lane)
        tiles(RING - 1, lambda step, lane=lane, parts=parts: scatter_small(lane, part_of(step), parts))

    for load in (load_mom, load_sec, load_srv):
        load.wait()
    shared = []
    for lane in range(LANES):
        begin, width = lanes[lane]
        columns = pl.ds(begin, width)
        parts = [(got1.at[lane, 0, message], got1_top.at[lane, 0, message]) for message in (1, 2)]
        parts += [(got2.at[lane, slot], got2_top.at[lane, slot]) for slot in range(RING - 1)]
        total = own_value(lane, parts, me[SCATTER[lane][2]])
        for slot in range(RING - 1):
            landed(small(lane, slot + 1))
            total += decoded(got3.at[lane, slot], got3_top.at[lane, slot], lane, 0)
        grad = scale * total
        first_new = beta_one * mom[:, columns] + (1.0 - beta_one) * grad
        squares_new = beta_two * sec[:, columns] + (1.0 - beta_two) * grad * grad
        step = first_new / bias_one / (jnp.sqrt(squares_new / bias_two) + epsilon)
        current = weights[me[0], me[1], me[2], :, columns].astype(jnp.float32)
        updated = current - learn_rate * (step + decay_rate * current)
        delta[core, :, columns] = (updated - current).astype(delta.dtype)
        part = delta.at[core, :, columns]
        shared.append(pltpu.make_async_remote_copy(
            src_ref=part, dst_ref=part, send_sem=d_send.at[lane], recv_sem=d_recv.at[lane],
            device_id={"expert": 1 - core}, device_id_type=MESH,
        ))
        shared[lane].start()
        nw[:, columns] = updated.astype(nw.dtype)
        nm[:, columns] = first_new
        ns[:, columns] = squares_new
    for lane in range(LANES):
        begin, width = lanes[lane]
        columns = pl.ds(begin, width)
        shared[lane].wait_recv()
        choices = [delta[expert, :, columns].astype(jnp.float32) for expert in range(2)]
        for replica in range(srv.shape[0]):
            pick = jnp.full((owned, width), placement[core, replica], jnp.int32) == 0
            incoming = jnp.where(pick, choices[0], choices[1])
            so[replica, :, columns] = (srv[replica, :, columns].astype(jnp.float32) + incoming).astype(so.dtype)

    def sent_all(k):
        for lane in every:
            for slot in range(3):
                gather_large(lane, k, slot).wait_send()
                gone(large(lane, k, slot))

            @pl.when(k > 0)
            def _():
                gather_small(lane, 0, k, ga_send, ga_recv).wait_send()
                gather_small(lane, 1, k, gb_send, gb_recv).wait_send()
                gone(medium(lane, k))
                gone(small(lane, k))
    tiles(RING, sent_all)
    for copy in shared:
        copy.wait_send()


def on_device(hidden, cotangent, counts, placement, weight, moment, second, serving):
    tokens, rows = hidden.shape[1:]
    width = cotangent.shape[2]
    owned = weight.shape[1]
    copies = serving.shape[1]
    gather_lanes = lane_columns(width, 0)
    lanes = lane_columns(width, 1)
    widest = max(count for _, count in lanes)
    scale = width ** (-0.5)
    anywhere = pl.BlockSpec(memory_space=pl.ANY)
    scalars = pl.BlockSpec(memory_space=pltpu.SMEM)
    f32, bf16, i16 = jnp.float32, jnp.bfloat16, jnp.int16
    dma = pltpu.SemaphoreType.DMA
    outs = pl.pallas_call(
        functools.partial(fused, scale, gather_lanes, lanes),
        out_shape=(
            pltpu.VMEM((tokens, rows), bf16),
            pltpu.VMEM((owned, width), bf16),
            pltpu.VMEM((owned, width), f32),
            pltpu.VMEM((owned, width), f32),
            pltpu.VMEM((copies, owned, width), bf16),
        ),
        in_specs=[scalars, scalars] + [anywhere] * 6,
        out_specs=[pl.BlockSpec(memory_space=pltpu.VMEM)] * 5,
        scratch_shapes=[
            pltpu.VMEM((RING, RING, RING, owned, width), bf16),
            pltpu.VMEM((tokens, rows), bf16),
            pltpu.VMEM((rows, tokens), bf16),
            pltpu.VMEM((tokens, width), bf16),
            pltpu.VMEM((RING, RING, RING, owned, width), f32),
            pltpu.VMEM((owned, width), f32),
            pltpu.VMEM((owned, width), f32),
            pltpu.VMEM((copies, owned, width), bf16),
            pltpu.VMEM((2, owned, width), bf16),
            pltpu.VMEM((LANES, RING, 3, RING, owned, widest), i16),
            pltpu.VMEM((LANES, RING, 3, RING, owned, widest), i16),
            pltpu.VMEM((LANES, 3, RING, owned, widest), i16),
            pltpu.VMEM((LANES, 3, RING, owned, widest), i16),
            pltpu.VMEM((LANES, 3, 1, owned, widest), i16),
            pltpu.VMEM((LANES, 3, 1, owned, widest), i16),
            pltpu.VMEM((LANES, RING, 3, 8, 128), f32),
            pltpu.VMEM((LANES, RING, 3, 8, 128), f32),
            pltpu.VMEM((LANES, 3, 8, 128), f32),
            pltpu.VMEM((LANES, 3, 8, 128), f32),
            pltpu.VMEM((LANES, 3, 8, 128), f32),
            pltpu.VMEM((LANES, 3, 8, 128), f32),
        ]
        + [dma((LANES, 3))] * 4
        + [dma((LANES, RING, 3))] * 6
        + [dma((LANES, 3))] * 8
        + [dma((LANES,))] * 2
        + [dma((6,))],
        compiler_params=pltpu.CompilerParams(
            collective_id=0, has_side_effects=True, vmem_limit_bytes=56 * 2**20
        ),
        cost_estimate=pl.CostEstimate(flops=4 * tokens * rows * width, bytes_accessed=2**25, transcendentals=0),
    )(counts, placement, hidden[0], cotangent[0], weight[0], moment[0], second[0], serving[0])
    return tuple(out[None] for out in outs)


def solution(mesh):
    torus = Mesh(
        mesh.devices.reshape(RING, RING, RING, mesh.shape["expert"]), ("dp_0", "dp_1", "dp_2", "expert")
    )
    return jax.shard_map(
        on_device,
        mesh=torus,
        in_specs=(
            P("expert", DP, None),
            P("expert", DP, None),
            P("expert", DP),
            P(),
            P("expert", DP, None),
            P("expert", DP, None),
            P("expert", DP, None),
            P("expert", None, DP, None),
        ),
        out_specs=(
            P("expert", DP, None),
            P("expert", DP, None),
            P("expert", DP, None),
            P("expert", DP, None),
            P("expert", None, DP, None),
        ),
        check_vma=False,
    )
```

time: 302 us -> 87.5 us (0.29)
  waiting for transfers between devices: 232 us -> 0 us
  Pallas kernels: 0 us -> 80.4 us
  matrix products: 27.6 us -> 0 us
  between operations: 16.1 us -> 1.29 us
  blocking collectives: 7.92 us -> 0 us
  local copies, waits for them, and re-layouts: 11.6 us -> 4.11 us
  other arithmetic: 5.8 us -> 0 us
    reduce_scatter x2 -> x0, waiting for transfers between devices: 134 us -> none  [summed_rows(): nearer = lax.psum_scatter(array, axes[0], scatter_dimension=dim, tiled=True)]
    pallas_call x0 -> x1, Pallas kernels: none -> 80.4 us  [on_device(): pl.pallas_call(functools.partial(fused, scale, gather_lanes, lanes), out_...]
    all_gather x1 -> x0, waiting for transfers between devices: 54.5 us -> none  [on_device(): lax.all_gather(matrix, DP, axis=0, tiled=True)]
    unnamed x5 -> x0, waiting for transfers between devices: 43 us -> none
    dot_general x2 -> x0, matrix products: 27.6 us -> none  [the longest x1 14.4 us: on_device(): jnp.dot(acts.T, masked, preferred_element_type=jnp.float32)]
    all_to_all x2 -> x0, blocking collectives: 7.92 us -> none  [the longest x1 4.1 us: on_device(): lax.all_to_all(chosen, 'expert', split_axis=1, concat_axis=1, tiled=True)]
    convert_element_type x2 -> x0, other arithmetic: 3.72 us -> none  [the longest x1 1.86 us: on_device(): (serving[0].astype(jnp.float32) + incoming.astype(jnp.float32)).astype(jn...]
    convert_element_type x2 -> x0, local copies, waits for them, and re-layouts: 3.39 us -> none  [on_device(): incoming.astype(jnp.float32)]
  transfers between devices with their start and end apart: 4 -> 0, of which waited for: 3 -> 0; matrix products, arithmetic and copies ran while one was open for 4% -> 0% of each run, Pallas kernels for 0% -> 0%
where the time goes in v2:
time: 87.5 us; the launch traced here: 85.8 us
  Pallas kernels  80.4 us (92%)
  local copies, waits for them, and re-layouts  4.11 us (5%)
  between operations  1.29 us (1%)
    pallas_call x1, Pallas kernels, on_device(): pl.pallas_call(functools.partial(fused, scale, gather_lanes, lanes), out_...  80.4 us
    unnamed x5, local copies, waits for them, and re-layouts  4.11 us

profile of v2, /device:TPU:0, one launch (start us, length us, event | category | flops | bytes accessed | tf_op | source)
XLA Modules:
  0.0 85.8 jit_solution(4355192024994916073)
XLA Ops:
  1.3 80.4 %shard_map.119 = (bf16[1024,1024]{1,0:T(8,128)(2,1)S(1)}, bf16[16,3584]{1,0:T(8,128)(2,1)S(1)}, f32[16,3584]{1,0:T(8,128)S(1)}, f32[16,3584]{1,0:T(8,128)S(1)}, bf16[4,16,3584]{2,1,0:T(8,128)(2,1)S(1)}) custom-call(s32[1,1]{1,0:T(1,128)S(6)} %copy.23.counts, s32[2,4]{1,0:T(2,128)} %placement.1, bf16[1024,1024]{1,0:T(8,128)(2,1)} %bitcast.17, ...), custom_call_target="tpu_custom_call" | custom-call | flops 15032385536 | bytes 33554432 | tf_op jit(solution)/shard_map/pallas_call | solution.py:398
  81.7 1.3 %copy.18 = bf16[1,1024,1024]{2,1,0:T(8,128)(2,1)} copy(bf16[1,1024,1024]{2,1,0:T(8,128)(2,1)S(1)} %bitcast.11) | data formatting | bytes 4194304
  83.0 0.6 copy.19
  83.7 0.7 copy.20
  84.3 0.7 copy.21
  85.0 0.8 copy.22

commit v3 on v2

--- a/solution.py
+++ b/solution.py
@@ -41,7 +41,7 @@
     scale, gather_lanes, lanes,
     counts, placement, hid_in, cot_in, w_in, mom_in, sec_in, srv_in,
     dh, nw, nm, ns, so,
-    weights, hid, hid_t, cot, grads, mom, sec, srv, delta,
+    weights, hid, hid_t, cot, grads, dh_t, mom, sec, srv, delta,
     sent1, got1, sent2, got2, sent3, got3,
     sent1_top, got1_top, sent2_top, got2_top, sent3_top, got3_top,
     ga_send, ga_recv, gb_send, gb_recv, gc_send, gc_recv,
@@ -68,6 +68,14 @@
         index = tuple(at.get(axis, slice(None)) for axis in range(3))
         return weights.at[index + (slice(None), pl.ds(*columns))]
 
+    barrier = pltpu.get_barrier_semaphore()
+    for axis in range(3):
+        for offset in range(1, RING):
+            pl.semaphore_signal(
+                barrier, inc=1, device_id={DP[axis]: on_ring(axis, offset)}, device_id_type=MESH
+            )
+    pl.semaphore_signal(barrier, inc=1, device_id={"expert": 1 - core}, device_id_type=MESH)
+
     load_w = pltpu.make_async_copy(w_in, weights.at[me[0], me[1], me[2]], in_sem.at[0])
     load_hid = pltpu.make_async_copy(hid_in, hid, in_sem.at[1])
     load_cot = pltpu.make_async_copy(cot_in, cot, in_sem.at[2])
@@ -77,13 +85,6 @@
     for load in (load_w, load_hid, load_cot, load_mom, load_sec, load_srv):
         load.start()
 
-    barrier = pltpu.get_barrier_semaphore()
-    for axis in range(3):
-        for offset in range(1, RING):
-            pl.semaphore_signal(
-                barrier, inc=1, device_id={DP[axis]: on_ring(axis, offset)}, device_id_type=MESH
-            )
-    pl.semaphore_signal(barrier, inc=1, device_id={"expert": 1 - core}, device_id_type=MESH)
     pl.semaphore_wait(barrier, 3 * (RING - 1) + 1)
 
     def tiles(count, body):
@@ -255,18 +256,39 @@
         )
         begin_all(small(lane, k))
 
+    def hidden_part(lane, offset):
+        axis = GATHER[lane][2]
+        columns = pl.ds(*gather_lanes[lane])
+        index = tuple(on_ring(axis, offset) if dim == axis else slice(None) for dim in range(3))
+        rows = weights[index + (slice(None), columns)].reshape(RING * RING * owned, gather_lanes[lane][1])
+        value = lax.dot_general(
+            rows, cot[:, columns], (((1,), (1,)), ((), ())), preferred_element_type=jnp.float32
+        )
+        dh_t[index] = dh_t[index] + value.reshape(RING, RING, owned, tokens)
+
     limit_mask = lax.broadcasted_iota(jnp.int32, (tokens, 1), 0) < limit
     quarter = RING * RING * owned
 
-    def d_hidden(at):
-        rows = weights[at].reshape(quarter, weights.shape[4])
-        value = lax.dot_general(
-            cot[...], rows, (((1,), (1,)), ((), ())), preferred_element_type=jnp.float32
-        )
-        value = jnp.where(limit_mask, scale * value, 0.0)
+    def turn_back(at):
+        value = scale * dh_t[at].reshape(quarter, tokens).T
+        value = jnp.where(limit_mask, value, 0.0)
         dh[:, pl.ds(pl.multiple_of(at * quarter, quarter), quarter)] = value.astype(dh.dtype)
 
     every = range(LANES)
+
+    def gather_next(k):
+        for slot in range(2):
+            for lane in every:
+                gather_large(lane, k, slot).start()
+
+    def gather_onward(k):
+        for lane in every:
+            gather_large(lane, k, 0).wait_recv()
+            gather_large(lane, k, 2).start()
+
+    def gather_middle(offset):
+        for lane in every:
+            gather_small(lane, 1, offset, gb_send, gb_recv).wait_recv()
 
     load_w.wait()
     for offset in (1, 3, 2):
@@ -274,23 +296,19 @@
             gather_small(lane, 0, offset, ga_send, ga_recv).start()
     load_hid.wait()
     tiles(tokens // TILE, turn)
+
+    def clear(at):
+        dh_t[at] = jnp.zeros(dh_t.shape[1:], jnp.float32)
+    tiles(RING, clear)
     for offset in (1, 3, 2):
         for lane in every:
             gather_small(lane, 0, offset, ga_send, ga_recv).wait_recv()
     for offset in (1, 3, 2):
         for lane in every:
             gather_small(lane, 1, offset, gb_send, gb_recv).start()
-    for slot in range(2):
-        for lane in every:
-            gather_large(lane, 0, slot).start()
+    gather_next(0)
     load_cot.wait()
     tiles(cot.shape[1] // TILE, product)
-    for offset in (3, 1, 2):
-        for lane in every:
-            gather_small(lane, 1, offset, gb_send, gb_recv).wait_recv()
-        for slot in range(2):
-            for lane in every:
-                gather_large(lane, RING - offset, slot).start()
 
     def near_and_far(step):
         k = part_of(step)
@@ -298,34 +316,32 @@
             scatter_large(lane, k, 0)
             scatter_large(lane, k, 1)
     tiles(RING, near_and_far)
-
-    def onward(step):
+    for offset in (1, 3, 2):
+        gather_middle(offset)
+    gather_next(1)
+    for lane in every:
+        hidden_part(lane, 0)
+
+    def with_far(step):
         k = part_of(step)
         for lane in every:
-            gather_large(lane, lax.rem(k + 2, RING), 0).wait_recv()
-            gather_large(lane, lax.rem(k + 2, RING), 2).start()
-        for lane in every:
             scatter_large(lane, k, 2)
-    tiles(RING, onward)
-
-    def gathered(k):
-        for lane in every:
-            gather_large(lane, k, 1).wait_recv()
-            gather_large(lane, k, 2).wait_recv()
-    tiles(RING, gathered)
-
-    def second_half(step):
-        d_hidden(step)
-
-        @pl.when(step < RING - 1)
-        def _():
-            k = part_of(step)
-            for lane in every:
-                scatter_middle(lane, k)
-    tiles(RING, second_half)
+    tiles(RING, with_far)
+    gather_next(3)
+    gather_onward(0)
+
+    def second_stage(step):
+        k = part_of(step)
+        for lane in every:
+            scatter_middle(lane, k)
+    tiles(RING - 1, second_stage)
+    gather_next(2)
     for lane in every:
         parts = own_parts(lane)
         tiles(RING - 1, lambda step, lane=lane, parts=parts: scatter_small(lane, part_of(step), parts))
+    gather_onward(1)
+    gather_onward(3)
+    gather_onward(2)
 
     for load in (load_mom, load_sec, load_srv):
         load.wait()
@@ -355,6 +371,14 @@
         nw[:, columns] = updated.astype(nw.dtype)
         nm[:, columns] = first_new
         ns[:, columns] = squares_new
+
+    def near_slab(step):
+        for lane in every:
+            hidden_part(lane, 1 + 2 * step)
+    for k in range(RING):
+        for lane in every:
+            gather_large(lane, k, 1).wait_recv()
+    tiles(2, near_slab)
     for lane in range(LANES):
         begin, width = lanes[lane]
         columns = pl.ds(begin, width)
@@ -365,6 +389,14 @@
             incoming = jnp.where(pick, choices[0], choices[1])
             so[replica, :, columns] = (srv[replica, :, columns].astype(jnp.float32) + incoming).astype(so.dtype)
 
+    def gathered(k):
+        for lane in every:
+            gather_large(lane, k, 2).wait_recv()
+    tiles(RING, gathered)
+    for lane in every:
+        hidden_part(lane, 2)
+    tiles(RING, turn_back)
+
     def sent_all(k):
         for lane in every:
             for slot in range(3):
@@ -380,6 +412,28 @@
     tiles(RING, sent_all)
     for copy in shared:
         copy.wait_send()
+
+
+def store(*refs):
+    count = len(refs) // 2
+    sem = refs[2 * count]
+    copies = [pltpu.make_async_copy(refs[at], refs[count + at], sem.at[at]) for at in range(count)]
+    for copy in copies:
+        copy.start()
+    for copy in copies:
+        copy.wait()
+
+
+def stored(arrays):
+    anywhere = pl.BlockSpec(memory_space=pl.ANY)
+    return pl.pallas_call(
+        store,
+        out_shape=tuple(jax.ShapeDtypeStruct(array.shape, array.dtype) for array in arrays),
+        in_specs=[anywhere] * len(arrays),
+        out_specs=[anywhere] * len(arrays),
+        scratch_shapes=[pltpu.SemaphoreType.DMA((len(arrays),))],
+        compiler_params=pltpu.CompilerParams(vmem_limit_bytes=2**20),
+    )(*arrays)
 
 
 def on_device(hidden, cotangent, counts, placement, weight, moment, second, serving):
@@ -412,6 +466,7 @@
             pltpu.VMEM((rows, tokens), bf16),
             pltpu.VMEM((tokens, width), bf16),
             pltpu.VMEM((RING, RING, RING, owned, width), f32),
+            pltpu.VMEM((RING, RING, RING, owned, tokens), f32),
             pltpu.VMEM((owned, width), f32),
             pltpu.VMEM((owned, width), f32),
             pltpu.VMEM((copies, owned, width), bf16),
@@ -439,7 +494,7 @@
         ),
         cost_estimate=pl.CostEstimate(flops=4 * tokens * rows * width, bytes_accessed=2**25, transcendentals=0),
     )(counts, placement, hidden[0], cotangent[0], weight[0], moment[0], second[0], serving[0])
-    return tuple(out[None] for out in outs)
+    return tuple(out[None] for out in stored(outs))
 
 
 def solution(mesh):

time: 87.5 us -> 82.2 us (0.939); the launches traced: 85.8 us -> 82 us
  local copies, waits for them, and re-layouts: 4.11 us -> 0 us
    unnamed x5 -> x0, local copies, waits for them, and re-layouts: 4.11 us -> none
    pallas_call x0 -> x1, Pallas kernels: none -> 1.69 us  [stored(): pl.pallas_call(store, out_shape=tuple((jax.ShapeDtypeStruct(array.shape,...]
    pallas_call x1, Pallas kernels: 80.4 us -> 79.1 us  [on_device(): pl.pallas_call(functools.partial(fused, scale, gather_lanes, lanes), out_...]
where the time goes in v3:
time: 82.2 us; the launch traced here: 82 us
  Pallas kernels  80.8 us (98%)
  between operations  1.29 us (2%)
    pallas_call x1, Pallas kernels, on_device(): pl.pallas_call(functools.partial(fused, scale, gather_lanes, lanes), out_...  79.1 us
    pallas_call x1, Pallas kernels, stored(): pl.pallas_call(store, out_shape=tuple((jax.ShapeDtypeStruct(array.shape,...  1.69 us

profile of v3, /device:TPU:0, one launch (start us, length us, event | category | flops | bytes accessed | tf_op | source)
XLA Modules:
  0.0 82.0 jit_solution(3706542113115486824)
XLA Ops:
  1.3 79.1 %shard_map.119 = (bf16[1024,1024]{1,0:T(8,128)(2,1)S(1)}, bf16[16,3584]{1,0:T(8,128)(2,1)S(1)}, f32[16,3584]{1,0:T(8,128)S(1)}, f32[16,3584]{1,0:T(8,128)S(1)}, bf16[4,16,3584]{2,1,0:T(8,128)(2,1)S(1)}) custom-call(s32[1,1]{1,0:T(1,128)S(6)} %copy.13.counts, s32[2,4]{1,0:T(2,128)} %placement.1, bf16[1024,1024]{1,0:T(8,128)(2,1)} %bitcast.12, ...), custom_call_target="tpu_custom_call" | custom-call | flops 15032385536 | bytes 33554432 | tf_op jit(solution)/shard_map/pallas_call | solution.py:452
  80.4 1.7 %shard_map.120 = (bf16[1024,1024]{1,0:T(8,128)(2,1)}, bf16[16,3584]{1,0:T(8,128)(2,1)}, f32[16,3584]{1,0:T(8,128)}, f32[16,3584]{1,0:T(8,128)}, bf16[4,16,3584]{2,1,0:T(8,128)(2,1)}) custom-call(bf16[1024,1024]{1,0:T(8,128)(2,1)S(1)} %get-tuple-element.15.refs_0_, bf16[16,3584]{1,0:T(8,128)(2,1)S(1)} %get-tuple-element.16.refs_1_, ...), custom_call_target="tpu_custom_call" | custom-call | tf_op jit(solution)/shard_map/pallas_call | solution.py:429

commit v4 on v3

--- a/solution.py
+++ b/solution.py
@@ -21,7 +21,7 @@
 epsilon = 1e-08
 
 TILE = 256
-TOP = 32767.0
+TOP = 32000.0
 LANES = 3
 GATHER = ((2, 1, 0), (0, 2, 1), (1, 0, 2))
 SCATTER = ((0, 1, 2), (1, 2, 0), (2, 0, 1))
@@ -43,11 +43,8 @@
     dh, nw, nm, ns, so,
     weights, hid, hid_t, cot, grads, dh_t, mom, sec, srv, delta,
     sent1, got1, sent2, got2, sent3, got3,
-    sent1_top, got1_top, sent2_top, got2_top, sent3_top, got3_top,
     ga_send, ga_recv, gb_send, gb_recv, gc_send, gc_recv,
-    r1_send, r1_recv, r1t_send, r1t_recv,
-    r2_send, r2_recv, r2t_send, r2t_recv,
-    r3_send, r3_recv, r3t_send, r3t_recv,
+    r1_send, r1_recv, r2_send, r2_recv, r3_send, r3_recv,
     d_send, d_recv, in_sem,
 ):
     me = tuple(lax.axis_index(name) for name in DP)
@@ -129,15 +126,37 @@
         at = {order[0]: first_at, order[1]: second_at, order[2]: third_at}
         return at[0], at[1], at[2]
 
-    def spread(tile, width):
-        rows = jnp.concatenate([tile] * (owned // 8), axis=0)
-        return jnp.concatenate([rows] * (width // 128), axis=1)
-
-    def decoded(codes, top_ref, lane, at):
-        width = lanes[lane][1]
-        return codes[at, :, pl.ds(0, width)].astype(jnp.float32) * spread(top_ref[...], width)
-
-    def encode(lane, where, count, parts, codes, top_ref):
+    def lane_tiles(lane):
+        return lanes[lane][1] // 128
+
+    def exponent_of(largest):
+        pieces = [largest[row : row + 8, column : column + 128]
+                  for row in range(0, owned, 8) for column in range(0, largest.shape[1], 128)]
+        while len(pieces) > 1:
+            pieces = [jnp.maximum(*pieces[at : at + 2]) if at + 1 < len(pieces) else pieces[at]
+                      for at in range(0, len(pieces), 2)]
+        exponent = jnp.ceil(jnp.log2(jnp.maximum(pieces[0], 1e-30)))
+        return jnp.concatenate([exponent] * (owned // 8), axis=0)
+
+    def spread(tile, lane):
+        return jnp.concatenate([tile] * lane_tiles(lane), axis=1)
+
+    def received(codes, count, lane):
+        exponent = codes[count * lane_tiles(lane)].astype(jnp.float32)
+        return codes, jnp.exp2(exponent) * (1.0 / TOP)
+
+    def decoded(part, lane, at):
+        codes, unit = part
+        count = lane_tiles(lane)
+        value = jnp.concatenate([codes[at * count + tile] for tile in range(count)], axis=1)
+        return value.astype(jnp.float32) * spread(unit, lane)
+
+    def put(codes, lane, at, scaled):
+        value = jnp.round(scaled).astype(jnp.int32).astype(jnp.int16)
+        for tile in range(lane_tiles(lane)):
+            codes[at * lane_tiles(lane) + tile] = value[:, tile * 128 : (tile + 1) * 128]
+
+    def encode(lane, where, count, parts, codes):
         begin, width = lanes[lane]
         columns = pl.ds(begin, width)
 
@@ -145,59 +164,32 @@
             index = where(at) + (slice(None), columns)
             value = grads[index]
             for part in parts:
-                value += decoded(part[0], part[1], lane, at)
+                value += decoded(part, lane, at)
             if parts:
                 grads[index] = value
             return jnp.maximum(top, jnp.abs(value))
-        top = lax.fori_loop(0, count, largest, jnp.zeros((owned, width), jnp.float32))
-        top = largest_piece(top)
-        factor = TOP / top
-        top_ref[...] = top * (1.0 / TOP)
+        exponent = exponent_of(lax.fori_loop(0, count, largest, jnp.zeros((owned, width), jnp.float32)))
+        codes[count * lane_tiles(lane)] = exponent.astype(jnp.int32).astype(jnp.int16)
+        factor = jnp.exp2(-exponent) * TOP
 
         def code(at):
-            value = grads[where(at) + (slice(None), columns)]
-            codes[at, :, pl.ds(0, width)] = jnp.round(value * spread(factor, width)).astype(jnp.int32).astype(jnp.int16)
+            put(codes, lane, at, grads[where(at) + (slice(None), columns)] * spread(factor, lane))
         tiles(count, code)
 
-    def code_copies(lane, slot, buffers, sems, axis, offset):
-        sent, sent_top, got, got_top = buffers
-        columns = pl.ds(0, lanes[lane][1])
-        return (
-            remote(sent_top.at[slot], got_top.at[slot], sems[2].at[slot], sems[3].at[slot], axis, offset),
-            remote(sent.at[slot + (slice(None), slice(None), columns)],
-                   got.at[slot + (slice(None), slice(None), columns)],
-                   sems[0].at[slot], sems[1].at[slot], axis, offset),
-        )
-
-    def begin_all(pair):
-        for copy in pair:
-            copy.start()
-
-    def landed(pair):
-        for copy in pair:
-            copy.wait_recv()
-
-    def gone(pair):
-        for copy in pair:
-            copy.wait_send()
-
-    buffers1 = (sent1, sent1_top, got1, got1_top)
-    buffers2 = (sent2, sent2_top, got2, got2_top)
-    buffers3 = (sent3, sent3_top, got3, got3_top)
-    sems1 = (r1_send, r1_recv, r1t_send, r1t_recv)
-    sems2 = (r2_send, r2_recv, r2t_send, r2t_recv)
-    sems3 = (r3_send, r3_recv, r3t_send, r3t_recv)
+    def code_copy(lane, slot, count, buffers, sems, axis, offset):
+        part = slot + (pl.ds(0, count * lane_tiles(lane) + 1),)
+        return remote(buffers[0].at[part], buffers[1].at[part], sems[0].at[slot], sems[1].at[slot], axis, offset)
 
     def large(lane, k, message):
         way = way_of(k)
-        return code_copies(lane, (lane, k, message), buffers1, sems1, SCATTER[lane][0],
-                           RING - way if message == 1 else way)
+        return code_copy(lane, (lane, k, message), RING, (sent1, got1), (r1_send, r1_recv), SCATTER[lane][0],
+                         RING - way if message == 1 else way)
 
     def medium(lane, k):
-        return code_copies(lane, (lane, k - 1), buffers2, sems2, SCATTER[lane][1], k)
+        return code_copy(lane, (lane, k - 1), RING, (sent2, got2), (r2_send, r2_recv), SCATTER[lane][1], k)
 
     def small(lane, k):
-        return code_copies(lane, (lane, k - 1), buffers3, sems3, SCATTER[lane][2], k)
+        return code_copy(lane, (lane, k - 1), 1, (sent3, got3), (r3_send, r3_recv), SCATTER[lane][2], k)
 
     def scatter_large(lane, k, message):
         order = SCATTER[lane]
@@ -206,55 +198,41 @@
         middle = on_ring(order[1], k)
         parts = []
         if message == 2:
-            landed(large(lane, k, 0))
-            parts = [(got1.at[lane, k, 0], got1_top.at[lane, k, 0])]
-        encode(lane, lambda at: place(order, row, middle, at), RING, parts,
-               sent1.at[lane, k, message], sent1_top.at[lane, k, message])
-        begin_all(large(lane, k, message))
+            large(lane, k, 0).wait_recv()
+            parts = [received(got1.at[lane, k, 0], RING, lane)]
+        encode(lane, lambda at: place(order, row, middle, at), RING, parts, sent1.at[lane, k, message])
+        large(lane, k, message).start()
 
     def near_parts(lane, k):
         for message in (1, 2):
-            landed(large(lane, k, message))
-        return [(got1.at[lane, k, message], got1_top.at[lane, k, message]) for message in (1, 2)]
+            large(lane, k, message).wait_recv()
+        return [received(got1.at[lane, k, message], RING, lane) for message in (1, 2)]
 
     def scatter_middle(lane, k):
         order = SCATTER[lane]
         middle = on_ring(order[1], k)
         encode(lane, lambda at: place(order, me[order[0]], middle, at), RING, near_parts(lane, k),
-               sent2.at[lane, k - 1], sent2_top.at[lane, k - 1])
-        begin_all(medium(lane, k))
+               sent2.at[lane, k - 1])
+        medium(lane, k).start()
 
     def own_parts(lane):
-        parts = near_parts(lane, 0)
         for k in range(1, RING):
-            landed(medium(lane, k))
-            parts.append((got2.at[lane, k - 1], got2_top.at[lane, k - 1]))
-        return parts
+            medium(lane, k).wait_recv()
+        return near_parts(lane, 0) + [received(got2.at[lane, slot], RING, lane) for slot in range(RING - 1)]
 
     def own_value(lane, parts, at):
         order = SCATTER[lane]
         value = grads[place(order, me[order[0]], me[order[1]], at) + (slice(None), pl.ds(*lanes[lane]))]
         for part in parts:
-            value += decoded(part[0], part[1], lane, at)
+            value += decoded(part, lane, at)
         return value
 
-    def largest_piece(top):
-        pieces = [top[row : row + 8, column : column + 128]
-                  for row in range(0, top.shape[0], 8) for column in range(0, top.shape[1], 128)]
-        while len(pieces) > 1:
-            pieces = [jnp.maximum(*pieces[at : at + 2]) if at + 1 < len(pieces) else pieces[at]
-                      for at in range(0, len(pieces), 2)]
-        return jnp.maximum(pieces[0], 1e-30)
-
     def scatter_small(lane, k, parts):
-        width = lanes[lane][1]
         value = own_value(lane, parts, on_ring(SCATTER[lane][2], k))
-        top = largest_piece(jnp.abs(value))
-        sent3_top[lane, k - 1] = top * (1.0 / TOP)
-        sent3[lane, k - 1, 0, :, pl.ds(0, width)] = (
-            jnp.round(value * spread(TOP / top, width)).astype(jnp.int32).astype(jnp.int16)
-        )
-        begin_all(small(lane, k))
+        exponent = exponent_of(jnp.abs(value))
+        sent3[lane, k - 1, lane_tiles(lane)] = exponent.astype(jnp.int32).astype(jnp.int16)
+        put(sent3.at[lane, k - 1], lane, 0, value * spread(jnp.exp2(-exponent) * TOP, lane))
+        small(lane, k).start()
 
     def hidden_part(lane, offset):
         axis = GATHER[lane][2]
@@ -315,19 +293,19 @@
         for lane in every:
             scatter_large(lane, k, 0)
             scatter_large(lane, k, 1)
+    gather_middle(3)
+    gather_next(1)
     tiles(RING, near_and_far)
-    for offset in (1, 3, 2):
+    for offset in (1, 2):
         gather_middle(offset)
-    gather_next(1)
+
+    def with_far(step):
+        k = part_of(step)
+        for lane in every:
+            scatter_large(lane, k, 2)
+    tiles(RING, with_far)
     for lane in every:
         hidden_part(lane, 0)
-
-    def with_far(step):
-        k = part_of(step)
-        for lane in every:
-            scatter_large(lane, k, 2)
-    tiles(RING, with_far)
-    gather_next(3)
     gather_onward(0)
 
     def second_stage(step):
@@ -335,6 +313,7 @@
         for lane in every:
             scatter_middle(lane, k)
     tiles(RING - 1, second_stage)
+    gather_next(3)
     gather_next(2)
     for lane in every:
         parts = own_parts(lane)
@@ -349,12 +328,12 @@
     for lane in range(LANES):
         begin, width = lanes[lane]
         columns = pl.ds(begin, width)
-        parts = [(got1.at[lane, 0, message], got1_top.at[lane, 0, message]) for message in (1, 2)]
-        parts += [(got2.at[lane, slot], got2_top.at[lane, slot]) for slot in range(RING - 1)]
+        parts = [received(got1.at[lane, 0, message], RING, lane) for message in (1, 2)]
+        parts += [received(got2.at[lane, slot], RING, lane) for slot in range(RING - 1)]
         total = own_value(lane, parts, me[SCATTER[lane][2]])
         for slot in range(RING - 1):
-            landed(small(lane, slot + 1))
-            total += decoded(got3.at[lane, slot], got3_top.at[lane, slot], lane, 0)
+            small(lane, slot + 1).wait_recv()
+            total += decoded(received(got3.at[lane, slot], 1, lane), lane, 0)
         grad = scale * total
         first_new = beta_one * mom[:, columns] + (1.0 - beta_one) * grad
         squares_new = beta_two * sec[:, columns] + (1.0 - beta_two) * grad * grad
@@ -389,29 +368,30 @@
             incoming = jnp.where(pick, choices[0], choices[1])
             so[replica, :, columns] = (srv[replica, :, columns].astype(jnp.float32) + incoming).astype(so.dtype)
 
+    def sent_all(k):
+        for lane in every:
+            for slot in range(2):
+                gather_large(lane, k, slot).wait_send()
+            for slot in range(3):
+                large(lane, k, slot).wait_send()
+
+            @pl.when(k > 0)
+            def _():
+                gather_small(lane, 0, k, ga_send, ga_recv).wait_send()
+                gather_small(lane, 1, k, gb_send, gb_recv).wait_send()
+                medium(lane, k).wait_send()
+                small(lane, k).wait_send()
+    tiles(RING, sent_all)
+    for copy in shared:
+        copy.wait_send()
+
     def gathered(k):
         for lane in every:
-            gather_large(lane, k, 2).wait_recv()
+            gather_large(lane, k, 2).wait()
     tiles(RING, gathered)
     for lane in every:
         hidden_part(lane, 2)
     tiles(RING, turn_back)
-
-    def sent_all(k):
-        for lane in every:
-            for slot in range(3):
-                gather_large(lane, k, slot).wait_send()
-                gone(large(lane, k, slot))
-
-            @pl.when(k > 0)
-            def _():
-                gather_small(lane, 0, k, ga_send, ga_recv).wait_send()
-                gather_small(lane, 1, k, gb_send, gb_recv).wait_send()
-                gone(medium(lane, k))
-                gone(small(lane, k))
-    tiles(RING, sent_all)
-    for copy in shared:
-        copy.wait_send()
 
 
 def store(*refs):
@@ -443,7 +423,7 @@
     copies = serving.shape[1]
     gather_lanes = lane_columns(width, 0)
     lanes = lane_columns(width, 1)
-    widest = max(count for _, count in lanes)
+    most = max(count for _, count in lanes) // 128
     scale = width ** (-0.5)
     anywhere = pl.BlockSpec(memory_space=pl.ANY)
     scalars = pl.BlockSpec(memory_space=pltpu.SMEM)
@@ -471,22 +451,16 @@
             pltpu.VMEM((owned, width), f32),
             pltpu.VMEM((copies, owned, width), bf16),
             pltpu.VMEM((2, owned, width), bf16),
-            pltpu.VMEM((LANES, RING, 3, RING, owned, widest), i16),
-            pltpu.VMEM((LANES, RING, 3, RING, owned, widest), i16),
-            pltpu.VMEM((LANES, 3, RING, owned, widest), i16),
-            pltpu.VMEM((LANES, 3, RING, owned, widest), i16),
-            pltpu.VMEM((LANES, 3, 1, owned, widest), i16),
-            pltpu.VMEM((LANES, 3, 1, owned, widest), i16),
-            pltpu.VMEM((LANES, RING, 3, 8, 128), f32),
-            pltpu.VMEM((LANES, RING, 3, 8, 128), f32),
-            pltpu.VMEM((LANES, 3, 8, 128), f32),
-            pltpu.VMEM((LANES, 3, 8, 128), f32),
-            pltpu.VMEM((LANES, 3, 8, 128), f32),
-            pltpu.VMEM((LANES, 3, 8, 128), f32),
+            pltpu.VMEM((LANES, RING, 3, RING * most + 1, owned, 128), i16),
+            pltpu.VMEM((LANES, RING, 3, RING * most + 1, owned, 128), i16),
+            pltpu.VMEM((LANES, 3, RING * most + 1, owned, 128), i16),
+            pltpu.VMEM((LANES, 3, RING * most + 1, owned, 128), i16),
+            pltpu.VMEM((LANES, 3, most + 1, owned, 128), i16),
+            pltpu.VMEM((LANES, 3, most + 1, owned, 128), i16),
         ]
         + [dma((LANES, 3))] * 4
-        + [dma((LANES, RING, 3))] * 6
-        + [dma((LANES, 3))] * 8
+        + [dma((LANES, RING, 3))] * 4
+        + [dma((LANES, 3))] * 4
         + [dma((LANES,))] * 2
         + [dma((6,))],
         compiler_params=pltpu.CompilerParams(

time: 82.2 us -> 80.7 us (0.982)
  Pallas kernels: 80.8 us -> 79.3 us
    pallas_call x1, Pallas kernels: 79.1 us -> 77.6 us  [on_device(): pl.pallas_call(functools.partial(fused, scale, gather_lanes, lanes), out_...]
where the time goes in v4:
time: 80.7 us; the launch traced here: 80.6 us
  Pallas kernels  79.3 us (98%)
  between operations  1.29 us (2%)
    pallas_call x1, Pallas kernels, on_device(): pl.pallas_call(functools.partial(fused, scale, gather_lanes, lanes), out_...  77.6 us
    pallas_call x1, Pallas kernels, stored(): pl.pallas_call(store, out_shape=tuple((jax.ShapeDtypeStruct(array.shape,...  1.69 us

profile of v4, /device:TPU:0, one launch (start us, length us, event | category | flops | bytes accessed | tf_op | source)
XLA Modules:
  0.0 80.6 jit_solution(6906790193919363232)
XLA Ops:
  1.3 77.6 %shard_map.119 = (bf16[1024,1024]{1,0:T(8,128)(2,1)S(1)}, bf16[16,3584]{1,0:T(8,128)(2,1)S(1)}, f32[16,3584]{1,0:T(8,128)S(1)}, f32[16,3584]{1,0:T(8,128)S(1)}, bf16[4,16,3584]{2,1,0:T(8,128)(2,1)S(1)}) custom-call(s32[1,1]{1,0:T(1,128)S(6)} %copy.13.counts, s32[2,4]{1,0:T(2,128)} %placement.1, bf16[1024,1024]{1,0:T(8,128)(2,1)} %bitcast.12, ...), custom_call_target="tpu_custom_call" | custom-call | flops 15032385536 | bytes 33554432 | tf_op jit(solution)/shard_map/pallas_call | solution.py:432
  78.9 1.7 %shard_map.120 = (bf16[1024,1024]{1,0:T(8,128)(2,1)}, bf16[16,3584]{1,0:T(8,128)(2,1)}, f32[16,3584]{1,0:T(8,128)}, f32[16,3584]{1,0:T(8,128)}, bf16[4,16,3584]{2,1,0:T(8,128)(2,1)}) custom-call(bf16[1024,1024]{1,0:T(8,128)(2,1)S(1)} %get-tuple-element.15.refs_0_, bf16[16,3584]{1,0:T(8,128)(2,1)S(1)} %get-tuple-element.16.refs_1_, ...), custom_call_target="tpu_custom_call" | custom-call | tf_op jit(solution)/shard_map/pallas_call | solution.py:409

commit v5 on v4

--- a/solution.py
+++ b/solution.py
@@ -101,6 +101,12 @@
         part = block({axis: me[axis] for axis in order[stage:]}, gather_lanes[lane])
         return remote(part, part, send.at[lane, offset - 1], recv.at[lane, offset - 1], order[stage], offset)
 
+    def gather_half(lane, half):
+        first, mid, axis = GATHER[lane]
+        way = (1, 3)[half]
+        part = block({first: pl.ds(2 * half, 2), mid: on_ring(mid, -way), axis: me[axis]}, gather_lanes[lane])
+        return remote(part, part, gb_send.at[lane, 1 + 2 * half], gb_recv.at[lane, 1 + 2 * half], mid, way)
+
     def gather_large(lane, k, slot):
         _, mid, axis = GATHER[lane]
         way = way_of(k)
@@ -108,6 +114,13 @@
         part = block({mid: on_ring(mid, k), axis: holder}, gather_lanes[lane])
         offset = RING - way if slot == 1 else way
         return remote(part, part, gc_send.at[lane, k, slot], gc_recv.at[lane, k, slot], axis, offset)
+
+    def gather_halves():
+        for half, offset in enumerate((1, 3)):
+            for lane in range(LANES):
+                gather_small(lane, 1, offset, gb_send, gb_recv).wait_recv()
+            for lane in range(LANES):
+                gather_half(lane, half).start()
 
     limit = counts[0, 0]
 
@@ -264,10 +277,6 @@
             gather_large(lane, k, 0).wait_recv()
             gather_large(lane, k, 2).start()
 
-    def gather_middle(offset):
-        for lane in every:
-            gather_small(lane, 1, offset, gb_send, gb_recv).wait_recv()
-
     load_w.wait()
     for offset in (1, 3, 2):
         for lane in every:
@@ -281,23 +290,30 @@
     for offset in (1, 3, 2):
         for lane in every:
             gather_small(lane, 0, offset, ga_send, ga_recv).wait_recv()
-    for offset in (1, 3, 2):
+    for offset in (1, 3):
         for lane in every:
             gather_small(lane, 1, offset, gb_send, gb_recv).start()
     gather_next(0)
     load_cot.wait()
-    tiles(cot.shape[1] // TILE, product)
+
+    def product_step(at):
+        product(at)
+
+        @pl.when(at == 5)
+        def _():
+            gather_halves()
+            gather_next(1)
+    tiles(cot.shape[1] // TILE, product_step)
 
     def near_and_far(step):
         k = part_of(step)
         for lane in every:
             scatter_large(lane, k, 0)
             scatter_large(lane, k, 1)
-    gather_middle(3)
-    gather_next(1)
     tiles(RING, near_and_far)
-    for offset in (1, 2):
-        gather_middle(offset)
+    for lane in every:
+        gather_half(lane, 0).wait_recv()
+        gather_half(lane, 1).wait_recv()
 
     def with_far(step):
         k = part_of(step)
@@ -378,10 +394,13 @@
             @pl.when(k > 0)
             def _():
                 gather_small(lane, 0, k, ga_send, ga_recv).wait_send()
-                gather_small(lane, 1, k, gb_send, gb_recv).wait_send()
                 medium(lane, k).wait_send()
                 small(lane, k).wait_send()
     tiles(RING, sent_all)
+    for lane in every:
+        for half, offset in enumerate((1, 3)):
+            gather_small(lane, 1, offset, gb_send, gb_recv).wait_send()
+            gather_half(lane, half).wait_send()
     for copy in shared:
         copy.wait_send()
 
@@ -458,7 +477,8 @@
             pltpu.VMEM((LANES, 3, most + 1, owned, 128), i16),
             pltpu.VMEM((LANES, 3, most + 1, owned, 128), i16),
         ]
-        + [dma((LANES, 3))] * 4
+        + [dma((LANES, 3))] * 2
+        + [dma((LANES, RING))] * 2
         + [dma((LANES, RING, 3))] * 4
         + [dma((LANES, 3))] * 4
         + [dma((LANES,))] * 2

time: 80.7 us -> 79.1 us (0.980)
  Pallas kernels: 79.3 us -> 77.7 us
    pallas_call x1, Pallas kernels: 77.6 us -> 76 us  [on_device(): pl.pallas_call(functools.partial(fused, scale, gather_lanes, lanes), out_...]
where the time goes in v5:
time: 79.1 us; the launch traced here: 79 us
  Pallas kernels  77.7 us (98%)
  between operations  1.29 us (2%)
    pallas_call x1, Pallas kernels, on_device(): pl.pallas_call(functools.partial(fused, scale, gather_lanes, lanes), out_...  76 us
    pallas_call x1, Pallas kernels, stored(): pl.pallas_call(store, out_shape=tuple((jax.ShapeDtypeStruct(array.shape,...  1.69 us

profile of v5, /device:TPU:0, one launch (start us, length us, event | category | flops | bytes accessed | tf_op | source)
XLA Modules:
  0.0 79.0 jit_solution(9416970158991652883)
XLA Ops:
  1.3 76.0 %shard_map.119 = (bf16[1024,1024]{1,0:T(8,128)(2,1)S(1)}, bf16[16,3584]{1,0:T(8,128)(2,1)S(1)}, f32[16,3584]{1,0:T(8,128)S(1)}, f32[16,3584]{1,0:T(8,128)S(1)}, bf16[4,16,3584]{2,1,0:T(8,128)(2,1)S(1)}) custom-call(s32[1,1]{1,0:T(1,128)S(6)} %copy.13.counts, s32[2,4]{1,0:T(2,128)} %placement.1, bf16[1024,1024]{1,0:T(8,128)(2,1)} %bitcast.12, ...), custom_call_target="tpu_custom_call" | custom-call | flops 15032385536 | bytes 33554432 | tf_op jit(solution)/shard_map/pallas_call | solution.py:451
  77.3 1.7 %shard_map.120 = (bf16[1024,1024]{1,0:T(8,128)(2,1)}, bf16[16,3584]{1,0:T(8,128)(2,1)}, f32[16,3584]{1,0:T(8,128)}, f32[16,3584]{1,0:T(8,128)}, bf16[4,16,3584]{2,1,0:T(8,128)(2,1)}) custom-call(bf16[1024,1024]{1,0:T(8,128)(2,1)S(1)} %get-tuple-element.15.refs_0_, bf16[16,3584]{1,0:T(8,128)(2,1)S(1)} %get-tuple-element.16.refs_1_, ...), custom_call_target="tpu_custom_call" | custom-call | tf_op jit(solution)/shard_map/pallas_call | solution.py:428

commit v6 on v5

--- a/solution.py
+++ b/solution.py
@@ -320,8 +320,6 @@
         for lane in every:
             scatter_large(lane, k, 2)
     tiles(RING, with_far)
-    for lane in every:
-        hidden_part(lane, 0)
     gather_onward(0)
 
     def second_stage(step):
@@ -331,6 +329,8 @@
     tiles(RING - 1, second_stage)
     gather_next(3)
     gather_next(2)
+    for lane in every:
+        hidden_part(lane, 0)
     for lane in every:
         parts = own_parts(lane)
         tiles(RING - 1, lambda step, lane=lane, parts=parts: scatter_small(lane, part_of(step), parts))

time: 79.1 us -> 79.1 us (level)
  no operation moved by 1% of the time
where the time goes in v6:
time: 79.1 us; the launch traced here: 79 us
  Pallas kernels  77.7 us (98%)
  between operations  1.29 us (2%)
    pallas_call x1, Pallas kernels, on_device(): pl.pallas_call(functools.partial(fused, scale, gather_lanes, lanes), out_...  76 us
    pallas_call x1, Pallas kernels, stored(): pl.pallas_call(store, out_shape=tuple((jax.ShapeDtypeStruct(array.shape,...  1.69 us

profile of v6, /device:TPU:0, one launch (start us, length us, event | category | flops | bytes accessed | tf_op | source)
XLA Modules:
  0.0 79.0 jit_solution(136837165707858859)
XLA Ops:
  1.3 76.0 %shard_map.119 = (bf16[1024,1024]{1,0:T(8,128)(2,1)S(1)}, bf16[16,3584]{1,0:T(8,128)(2,1)S(1)}, f32[16,3584]{1,0:T(8,128)S(1)}, f32[16,3584]{1,0:T(8,128)S(1)}, bf16[4,16,3584]{2,1,0:T(8,128)(2,1)S(1)}) custom-call(s32[1,1]{1,0:T(1,128)S(6)} %copy.13.counts, s32[2,4]{1,0:T(2,128)} %placement.1, bf16[1024,1024]{1,0:T(8,128)(2,1)} %bitcast.12, ...), custom_call_target="tpu_custom_call" | custom-call | flops 15032385536 | bytes 33554432 | tf_op jit(solution)/shard_map/pallas_call | solution.py:451
  77.3 1.7 %shard_map.120 = (bf16[1024,1024]{1,0:T(8,128)(2,1)}, bf16[16,3584]{1,0:T(8,128)(2,1)}, f32[16,3584]{1,0:T(8,128)}, f32[16,3584]{1,0:T(8,128)}, bf16[4,16,3584]{2,1,0:T(8,128)(2,1)}) custom-call(bf16[1024,1024]{1,0:T(8,128)(2,1)S(1)} %get-tuple-element.15.refs_0_, bf16[16,3584]{1,0:T(8,128)(2,1)S(1)} %get-tuple-element.16.refs_1_, ...), custom_call_target="tpu_custom_call" | custom-call | tf_op jit(solution)/shard_map/pallas_call | solution.py:428
